TPU v7x, 128 devices: a whole 4x4x4 slice. The times are simulated.
128 devices in a mesh: rows: 128 (over z, x, y, core).
Axes of the slice: x: 4, y: 4, z: 4, core: 2. Of those that a mesh axis runs over, the one named last changes fastest.
Arguments:
- covariates: float32 [262144, 128], P('rows'), may hold values from -24 to 24
- outcome: float32 [262144], P('rows'), may hold values from 0 to 3
- predictor: float32 [262144], P('rows'), may hold values from -1.5 to 1.5
- firm_id: int32 [262144], P('rows'), may hold values from 0 to 127
- dy_id: int32 [262144], P('rows'), may hold values from 0 to 2047
- pd_owner: int32 [262144, 1], P('rows'), may hold values from 0 to 127; in each aligned block of 2048 rows (0 to 2047, 2048 to 4095, ...) at most 32 rows name the same one
- pd_local: int32 [262144], P('rows'), may hold values from 0 to 15
Outputs:
- x_tilde: float32 [262144, 128], P('rows')
- z_tilde: float32 [262144], P('rows')
- gram: float32 [128, 128], P('rows')
- rhs: float32 [128], P('rows')
Inputs may be any that keep to these rules, and one draw needn't show every extreme that they name: `pd_owner`: among the rows of one device no owner is named more than 32 times, a bound that some block reaches.
All inputs are finite; a program needn't handle non-finite values.
Results may differ from a plain program's by a relative error of at most 0.0003.
Values sent between devices are 32-bit elements; how exact they have to be, the bound alone decides.
A program may use at most 64 MiB of HBM per device.

v0:
```python
import math

import jax
import jax.numpy as jnp
from jax import lax
from jax.sharding import PartitionSpec as P

DY = 2048
FIRM_DEV = 128
PD_DEV = 16


def block_length(rows, segments):
    target = max(128, 1048576 // segments)
    return math.gcd(rows, target)


def onehot_sums(values, groups, segments):
    rows = values.shape[0]
    columns = values.shape[1]
    step = block_length(rows, segments)
    blocks = rows // step
    value_blocks = values.reshape(blocks, step, columns)
    group_blocks = groups.reshape(blocks, step)
    labels = jnp.arange(segments, dtype=jnp.int32)

    def accumulate(total, pair):
        block_values, block_groups = pair
        table = (block_groups[:, None] == labels[None, :]).astype(jnp.float32)
        added = jnp.dot(
            table.T,
            block_values,
            precision=lax.Precision.HIGHEST,
            preferred_element_type=jnp.float32,
        )
        return (total + added, None)

    start = jnp.zeros((segments, columns), jnp.float32)
    total, unused = lax.scan(accumulate, start, (value_blocks, group_blocks))
    return total


def onehot_pick(table, groups):
    rows = groups.shape[0]
    segments = table.shape[0]
    columns = table.shape[1]
    step = block_length(rows, segments)
    blocks = rows // step
    group_blocks = groups.reshape(blocks, step)
    labels = jnp.arange(segments, dtype=jnp.int32)

    def pick(carry, block_groups):
        selector = (block_groups[:, None] == labels[None, :]).astype(jnp.float32)
        picked = jnp.dot(
            selector, table, precision=lax.Precision.HIGHEST, preferred_element_type=jnp.float32
        )
        return (carry, picked)

    unused, picked = lax.scan(pick, jnp.int32(0), group_blocks)
    return picked.reshape(rows, columns)


def weighted_columns(covariates, working, weight):
    return jnp.concatenate(
        [weight[:, None] * covariates, (weight * working)[:, None], weight[:, None]], axis=1
    )


def split_sums(sums, width):
    return (sums[:, :width], sums[:, width], sums[:, width + 1])


def group_means(sum_x, sum_z, sum_w):
    denominator = jnp.where(sum_w > 0.0, sum_w, jnp.float32(1.0))
    return (sum_x / denominator[:, None], sum_z / denominator)


def subtract_means(covariates, working, mean_x, mean_z, groups):
    table = jnp.concatenate([mean_x, mean_z[:, None]], axis=1)
    picked = onehot_pick(table, groups)
    width = covariates.shape[1]
    return (covariates - picked[:, :width], working - picked[:, width])


def shards(covariates, outcome, predictor, firm_id, dy_id, pd_owner, pd_local):
    rows_dev = covariates.shape[0]
    width = covariates.shape[1]
    devices = lax.axis_size("rows")
    weight = jnp.exp(predictor)
    working = predictor + outcome / weight - 1.0
    sums = onehot_sums(weighted_columns(covariates, working, weight), firm_id, FIRM_DEV)
    mean_x, mean_z = group_means(*split_sums(sums, width))
    covariates, working = subtract_means(covariates, working, mean_x, mean_z, firm_id)
    sums = onehot_sums(weighted_columns(covariates, working, weight), dy_id, DY)
    sum_x, sum_z, sum_w = split_sums(sums, width)
    sum_x, sum_z, sum_w = lax.psum((sum_x, sum_z, sum_w), "rows")
    mean_x, mean_z = group_means(sum_x, sum_z, sum_w)
    covariates, working = subtract_means(covariates, working, mean_x, mean_z, dy_id)
    owners = pd_owner[:, 0]
    capacity = 2 * rows_dev // devices
    owner_labels = jnp.arange(devices, dtype=jnp.int32)
    owner_table = (owners[:, None] == owner_labels[None, :]).astype(jnp.int32)
    running = jnp.cumsum(owner_table, axis=0)
    position = jnp.sum(owner_table * (running - 1), axis=1)
    slot_of = owners * capacity + position
    slot_total = devices * capacity
    packed = jnp.concatenate(
        [weighted_columns(covariates, working, weight), pd_local.astype(jnp.float32)[:, None]],
        axis=1,
    )
    send_all = onehot_sums(packed, slot_of, slot_total)
    send_x = send_all[:, :width]
    send_zw = send_all[:, width : width + 2]
    send_ids = send_all[:, width + 2].astype(jnp.int32)
    arrived_ids = lax.all_to_all(send_ids, "rows", split_axis=0, concat_axis=0, tiled=True)
    arrived_x, arrived_zw = (
        lax.all_to_all(send_x, "rows", split_axis=0, concat_axis=0, tiled=True),
        lax.all_to_all(send_zw, "rows", split_axis=0, concat_axis=0, tiled=True),
    )
    owner_sums = onehot_sums(jnp.concatenate([arrived_x, arrived_zw], axis=1), arrived_ids, PD_DEV)
    mean_x, mean_z = group_means(*split_sums(owner_sums, width))
    mean_table = jnp.concatenate([mean_x, mean_z[:, None]], axis=1)
    per_slot = onehot_pick(mean_table, arrived_ids)
    back_x, back_z = (
        lax.all_to_all(per_slot[:, :width], "rows", split_axis=0, concat_axis=0, tiled=True),
        lax.all_to_all(per_slot[:, width], "rows", split_axis=0, concat_axis=0, tiled=True),
    )
    returned = onehot_pick(jnp.concatenate([back_x, back_z[:, None]], axis=1), slot_of)
    covariates = covariates - returned[:, :width]
    working = working - returned[:, width]
    scaled = weight[:, None] * covariates
    gram_term = jnp.dot(scaled.T, covariates, precision=lax.Precision.HIGHEST)
    rhs_term = jnp.dot(scaled.T, working, precision=lax.Precision.HIGHEST)
    total_rows = rows_dev * devices
    gram_all, rhs_all = lax.psum((gram_term, rhs_term), "rows")
    share = width // devices
    first_row = lax.axis_index("rows") * share
    gram_part = lax.dynamic_slice_in_dim(gram_all, first_row, share, 0)
    rhs_part = lax.dynamic_slice_in_dim(rhs_all, first_row, share, 0)
    return (covariates, working, gram_part / total_rows, rhs_part / total_rows)


def solution(mesh):
    in_specs = (
        P("rows", None),
        P("rows"),
        P("rows"),
        P("rows"),
        P("rows"),
        P("rows", None),
        P("rows"),
    )
    out_specs = (P("rows", None), P("rows"), P("rows", None), P("rows"))
    return jax.shard_map(shards, mesh=mesh, in_specs=in_specs, out_specs=out_specs, check_vma=False)
```

profile of v0, /device:TPU:1, one launch (start us, length us, event | category | flops | bytes accessed | tf_op | source)
XLA Modules:
  0.0 629.4 jit_solution(8959829769364204124)
XLA Ops:
  19.0 7.7 %while.14 = (s32[]{:T(128)}, f32[2048,130]{0,1:T(8,128)S(1)}, s32[4,512]{1,0:T(4,128)S(1)}, f32[4,512,130]{2,1,0:T(8,128)S(1)}, s32[]{:T(128)}, /*index=5*/s32[]{:T(128)}) while((s32[]{:T(128)}, f32[2048,130]{0,1:T(8,128)S(1)}, s32[4,512]{1,0:T(4,128)S(1)}, f32[4,512,130]{2,1,0:T(8,128)S(1)}, s32[]{:T(128)}, ...), condition=%wide.region_1.2_spmd.clone, body=%wide.region_0.1_spmd.clone.sunk | while | flops 1637359616 | bytes 2709591 | solution.py:39
  35.4 70.0 %all-reduce = (f32[2048]{0:T(1024)S(1)}, f32[2048]{0:T(1024)S(1)}) all-reduce(f32[2048]{0:T(1024)S(1)} %bitcast.117, f32[2048]{0:T(1024)S(1)} %bitcast.116), channel_id=1, replica_groups=mesh['rows'=128] {'rows'}, use_global_device_ids=true, to_apply=%region_4.5 | all-reduce | flops 4096 | bytes 32768 | tf_op jit(solution)/shard_map/psum | solution.py:96
  105.4 74.1 %all-reduce.4.cloned.1.call-done = f32[2048,128]{0,1:T(8,128)} async-done(((f32[2048,128]{0,1:T(8,128)}), f32[2048,128]{0,1:T(8,128)}) %all-reduce.4.cloned.1.call-update) | async-done | bytes 1048592 | tf_op jit(solution)/shard_map/psum | solution.py:96
  182.7 43.4 %while.12 = (s32[]{:T(128)}, f32[4,512,129]{1,0,2:T(4,128)}, s32[4,512]{1,0:T(4,128)S(1)}, f32[2048,129]{1,0:T(8,128)}, s32[]{:T(128)}, /*index=5*/s32[]{:T(128)}) while((s32[]{:T(128)}, f32[4,512,129]{1,0,2:T(4,128)}, s32[4,512]{1,0:T(4,128)S(1)}, f32[2048,129]{1,0:T(8,128)}, s32[]{:T(128)}, /*index=5*/s32[]{:T(128)}) %tuple.112), condition=%wide.region_6.7_spmd.clone, body=%wide.region_5.6_spmd.clone.sunk | while | flops 1624244224 | bytes 2383949 | solution.py:59
  187.1 6.4 %dynamic_update_slice.18 = f32[4,512,129]{1,0,2:T(4,128)} dynamic-update-slice(f32[4,512,129]{1,0,2:T(4,128)} %get-tuple-element.431, f32[1,512,129]{1,0,2:T(1,128)S(1)} %copy.98, s32[]{:T(128)} %get-tuple-element.430, s32[]{:T(128)} %constant.73.clone.1..sunk, s32[]{:T(128)} %constant.73.clone.1..sunk) | dynamic-update-slice | bytes 528388 | tf_op jit(solution)/shard_map/while/body/jit(dynamic_update_index_in_dim)/dynamic_update_slice | solution.py:59
  198.0 6.4 %dynamic_update_slice.18 = f32[4,512,129]{1,0,2:T(4,128)} dynamic-update-slice(f32[4,512,129]{1,0,2:T(4,128)} %get-tuple-element.431, f32[1,512,129]{1,0,2:T(1,128)S(1)} %copy.98, s32[]{:T(128)} %get-tuple-element.430, s32[]{:T(128)} %constant.73.clone.1..sunk, s32[]{:T(128)} %constant.73.clone.1..sunk) | dynamic-update-slice | bytes 528388 | tf_op jit(solution)/shard_map/while/body/jit(dynamic_update_index_in_dim)/dynamic_update_slice | solution.py:59
  208.8 6.4 %dynamic_update_slice.18 = f32[4,512,129]{1,0,2:T(4,128)} dynamic-update-slice(f32[4,512,129]{1,0,2:T(4,128)} %get-tuple-element.431, f32[1,512,129]{1,0,2:T(1,128)S(1)} %copy.98, s32[]{:T(128)} %get-tuple-element.430, s32[]{:T(128)} %constant.73.clone.1..sunk, s32[]{:T(128)} %constant.73.clone.1..sunk) | dynamic-update-slice | bytes 528388 | tf_op jit(solution)/shard_map/while/body/jit(dynamic_update_index_in_dim)/dynamic_update_slice | solution.py:59
  219.7 6.4 %dynamic_update_slice.18 = f32[4,512,129]{1,0,2:T(4,128)} dynamic-update-slice(f32[4,512,129]{1,0,2:T(4,128)} %get-tuple-element.431, f32[1,512,129]{1,0,2:T(1,128)S(1)} %copy.98, s32[]{:T(128)} %get-tuple-element.430, s32[]{:T(128)} %constant.73.clone.1..sunk, s32[]{:T(128)} %constant.73.clone.1..sunk) | dynamic-update-slice | bytes 528388 | tf_op jit(solution)/shard_map/while/body/jit(dynamic_update_index_in_dim)/dynamic_update_slice | solution.py:59
  238.0 29.0 %while.15 = (s32[]{:T(128)}, f32[4096,131]{0,1:T(8,128)S(1)}, s32[8,256]{1,0:T(8,128)S(1)}, f32[8,256,131]{2,1,0:T(8,128)}, s32[]{:T(128)}, /*index=5*/s32[]{:T(128)}) while((s32[]{:T(128)}, f32[4096,131]{0,1:T(8,128)S(1)}, s32[8,256]{1,0:T(8,128)S(1)}, f32[8,256,131]{2,1,0:T(8,128)}, s32[]{:T(128)}, ...), condition=%wide.region_11.12_spmd.clone, body=%wide.region_10.11_spmd.clone.sunk | while | flops 1650483200 | bytes 4558419 | solution.py:39
  267.7 6.8 %all-to-all-start = ((s32[128,32,1]{1,2,0:T(1,128)}), s32[128,32,1]{1,2,0:T(1,128)S(1)}, u32[]{:S(2)}, u32[]{:S(2)}) async-start(s32[128,32,1]{1,2,0:T(1,128)} %bitcast.15), calls=%async_computation | async-start | bytes 131072 | tf_op jit(solution)/shard_map/all_to_all | solution.py:115
  275.4 8.7 %all-to-all-done = s32[128,32,1]{1,2,0:T(1,128)S(1)} async-done(((s32[128,32,1]{1,2,0:T(1,128)}), s32[128,32,1]{1,2,0:T(1,128)S(1)}, u32[]{:S(2)}, u32[]{:S(2)}) %all-to-all-start) | async-done | bytes 16416 | tf_op jit(solution)/shard_map/all_to_all | solution.py:115
  298.6 6.1 all-to-all-start.1
  308.2 26.5 %all-to-all-done.1 = f32[128,32,128]{2,1,0:T(8,128)S(1)} async-done(((f32[128,32,128]{2,1,0:T(8,128)}), f32[128,32,128]{2,1,0:T(8,128)S(1)}, u32[]{:S(2)}, u32[]{:S(2)}) %all-to-all-start.1) | async-done | bytes 2097184 | tf_op jit(solution)/shard_map/all_to_all | solution.py:117
  363.9 25.2 %all-to-all-done.3 = f32[128,32,128]{2,1,0:T(8,128)S(1)} async-done(((f32[128,32,128]{2,1,0:T(8,128)}), f32[128,32,128]{2,1,0:T(8,128)S(1)}, u32[]{:S(2)}, u32[]{:S(2)}) %all-to-all-start.3) | async-done | bytes 2097184 | tf_op jit(solution)/shard_map/all_to_all | solution.py:125
  392.9 87.4 %while.13 = (s32[]{:T(128)}, f32[8,256,129]{1,0,2:T(8,128)}, s32[8,256]{1,0:T(8,128)}, f32[4096,129]{1,0:T(8,128)}, s32[]{:T(128)}, /*index=5*/s32[]{:T(128)}) while((s32[]{:T(128)}, f32[8,256,129]{1,0,2:T(8,128)}, s32[8,256]{1,0:T(8,128)}, f32[4096,129]{1,0:T(8,128)}, s32[]{:T(128)}, /*index=5*/s32[]{:T(128)}) %tuple.113), condition=%wide.region_13.14_spmd.clone, body=%wide.region_12.13_spmd.clone.sunk | while | flops 1624244224 | bytes 2777165 | solution.py:59
  404.5 5.7 fusion.80
  415.5 5.7 fusion.80
  426.4 5.7 fusion.80
  437.3 5.7 fusion.80
  448.2 5.7 fusion.80
  459.1 5.7 fusion.80
  470.1 5.7 fusion.80
  486.9 63.4 %psum.39 = f32[128]{0:T(128)S(1)} all-reduce(f32[128]{0:T(128)S(1)} %convolution_bitcast_fusion), channel_id=1, replica_groups=mesh['rows'=128] {'rows'}, use_global_device_ids=true, to_apply=%region_15.16 | all-reduce | flops 128 | bytes 1024 | tf_op jit(solution)/shard_map/psum | solution.py:135
  551.5 68.7 %all-reduce.6.cloned.1.call-done = f32[128,128]{1,0:T(8,128)} async-done(((f32[128,128]{1,0:T(8,128)}), f32[128,128]{1,0:T(8,128)}) %all-reduce.6.cloned.1.call-update) | async-done | bytes 65552 | tf_op jit(solution)/shard_map/psum | solution.py:135
  (191 shorter events, 197.1 us)
Async XLA Ops:
  7.2 1.6 copy-start.10
  7.2 1.6 copy-start.8
  7.2 1.8 copy-start.17
  7.2 172.3 %all-reduce.4.cloned.1.call-start = ((), (), s32[]{:S(2)}) async-start(), calls=%async_computation.5 | async-start | bytes 2097152 | tf_op jit(solution)/shard_map/psum | solution.py:96
  8.8 1.9 copy-start
  10.7 1.0 copy-start.2
  11.7 5.0 copy-start.18
  26.7 3.0 copy-start.19
  27.7 3.8 copy-start.12
  32.0 1.0 copy-start.7
  226.1 2.0 copy-start.1
  226.1 2.0 copy-start.3
  228.1 1.3 copy-start.5
  229.4 8.6 %copy-start.13 = (f32[2048,1]{0,1:T(1,128)}, f32[2048,1]{0,1:T(1,128)S(1)}, u32[]{:S(2)}) copy-start(f32[2048,1]{0,1:T(1,128)S(1)} %slice.96) | copy-start | bytes 24580
  267.0 7.6 %copy-start.15 = (s32[8,256]{1,0:T(8,128)}, s32[8,256]{1,0:T(8,128)S(1)}, u32[]{:S(2)}) copy-start(s32[8,256]{1,0:T(8,128)S(1)} %get-tuple-element.493) | copy-start | bytes 24580
  267.7 16.4 %all-to-all-start = ((s32[128,32,1]{1,2,0:T(1,128)}), s32[128,32,1]{1,2,0:T(1,128)S(1)}, u32[]{:S(2)}, u32[]{:S(2)}) async-start(s32[128,32,1]{1,2,0:T(1,128)} %bitcast.15), calls=%async_computation | async-start | bytes 131072 | tf_op jit(solution)/shard_map/all_to_all | solution.py:115
  284.2 14.4 %all-to-all-start.2 = ((f32[128,32,2]{1,2,0:T(2,128)}), f32[128,32,2]{1,2,0:T(2,128)S(1)}, u32[]{:S(2)}, u32[]{:S(2)}) async-start(f32[128,32,2]{1,2,0:T(2,128)} %copy.78), calls=%async_computation.2 | async-start | bytes 262144 | tf_op jit(solution)/shard_map/all_to_all | solution.py:118
  298.6 36.2 %all-to-all-start.1 = ((f32[128,32,128]{2,1,0:T(8,128)}), f32[128,32,128]{2,1,0:T(8,128)S(1)}, u32[]{:S(2)}, u32[]{:S(2)}) async-start(f32[128,32,128]{2,1,0:T(8,128)} %bitcast.16), calls=%async_computation.1 | async-start | bytes 4194304 | tf_op jit(solution)/shard_map/all_to_all | solution.py:117
  340.0 14.4 %all-to-all-start.4 = ((f32[128,32,1]{1,2,0:T(1,128)}), f32[128,32,1]{1,2,0:T(1,128)S(1)}, u32[]{:S(2)}, u32[]{:S(2)}) async-start(f32[128,32,1]{1,2,0:T(1,128)} %bitcast.21), calls=%async_computation.4 | async-start | bytes 131072 | tf_op jit(solution)/shard_map/all_to_all | solution.py:126
  354.4 34.7 %all-to-all-start.3 = ((f32[128,32,128]{2,1,0:T(8,128)}), f32[128,32,128]{2,1,0:T(8,128)S(1)}, u32[]{:S(2)}, u32[]{:S(2)}) async-start(f32[128,32,128]{2,1,0:T(8,128)} %bitcast.19), calls=%async_computation.3 | async-start | bytes 4194304 | tf_op jit(solution)/shard_map/all_to_all | solution.py:125
  359.0 261.2 %all-reduce.6.cloned.1.call-start = ((), (), s32[]{:S(2)}) async-start(), calls=%async_computation.6 | async-start | bytes 131072 | tf_op jit(solution)/shard_map/psum | solution.py:135
  480.3 1.9 copy-start.4
  480.3 1.9 copy-start.6
  482.9 3.9 copy-start.16
  (3 other events, 2.1 us)
Sparse Core Ops, SparseCore 0:
  27.9 151.5 all-reduce.3
  484.7 135.4 all-reduce.5
where the time goes:
time: 633 us; the launch traced here: 629 us
  waiting for transfers between devices  212 us (33%)
  blocking collectives  133 us (21%)
  local copies, waits for them, and re-layouts  114 us (18%)
  matrix products  107 us (17%)
  starting transfers between devices  26.6 us (4%)
  other arithmetic  19 us (3%)
  between operations  16.3 us (3%)
    psum x1, waiting for transfers between devices, shards(): sum_x, sum_z, sum_w = lax.psum((sum_x, sum_z, sum_w), 'rows')  74.1 us
    psum x1, blocking collectives, shards(): sum_x, sum_z, sum_w = lax.psum((sum_x, sum_z, sum_w), 'rows')  70 us
    psum x1, waiting for transfers between devices, shards(): gram_all, rhs_all = lax.psum((gram_term, rhs_term), 'rows')  68.7 us
    dot_general x14, matrix products, pick(): jnp.dot(selector, table, precision=lax.Precision.HIGHEST, preferred_eleme...  64.3 us
    psum x1, blocking collectives, shards(): gram_all, rhs_all = lax.psum((gram_term, rhs_term), 'rows')  63.4 us
    dynamic_update_slice x24, local copies, waits for them, and re-layouts, onehot_pick(): unused, picked = lax.scan(pick, jnp.int32(0), group_blocks)  62.7 us
    dot_general x14, matrix products, accumulate(): jnp.dot(table.T, block_values, precision=lax.Precision.HIGHEST, preferred...  40.1 us
    all_to_all x1, waiting for transfers between devices, shards(): lax.all_to_all(send_x, 'rows', split_axis=0, concat_axis=0, tiled=True)  26.5 us
  transfers between devices with their start and end apart: 7, of which 7 were waited for; matrix products, arithmetic and copies ran while one was open for 5% of the time, Pallas kernels for 0%

commit v1 on v0

v1 whole, which is shorter than its diff:
```python
import functools

import jax
import jax.numpy as jnp
from jax import lax
from jax.experimental import pallas as pl
from jax.experimental.pallas import tpu as pltpu
from jax.sharding import PartitionSpec as P

MESH = pl.DeviceIdType.MESH
F32 = jnp.float32
BF16 = jnp.bfloat16
I32 = jnp.int32
R = 2048
K = 128
NT = (((1,), (1,)), ((), ()))


def iota(shape, dim):
    return lax.broadcasted_iota(I32, shape, dim)


def split2(v):
    hi = v.astype(BF16)
    return hi, (v - hi.astype(F32)).astype(BF16)


def split3(v):
    hi = v.astype(BF16)
    rest = v - hi.astype(F32)
    mid = rest.astype(BF16)
    return hi, mid, (rest - mid.astype(F32)).astype(BF16)


def dot(a, b):
    return jnp.dot(a, b, preferred_element_type=F32)


def dot_nt(a, b):
    return lax.dot_general(a, b, NT, preferred_element_type=F32)


def blk(i, n=128):
    return slice(i * n, (i + 1) * n)


def kernel(total_rows, x_ref, out_r, pred_r, firm_r, dy_r, po_r, pl_r, pred_s, firm_s, dy_s, po_s, pl_s,
           xt_ref, zt_ref, gram_ref, rhs_ref, s):
    me = lax.axis_index("rows")
    c = lax.rem(me, 2)
    y = lax.rem(lax.div(me, 2), 4)
    x = lax.rem(lax.div(me, 8), 4)
    z = lax.div(me, 32)
    p = x + c * (y - x)
    q = y + c * (x - y)
    axis_p = (p, 8 - 6 * c)
    axis_q = (q, 2 + 6 * c)
    axis_z = (z, 32)
    partner = me + 1 - 2 * c
    mine = 64 * c
    theirs = 64 - mine

    def around(axis, k):
        u, stride = axis
        j = lax.rem(u + k, 4)
        return me + (j - u) * stride, j

    counter = [0]
    sends = []

    def sem(n=1):
        first = counter[0]
        counter[0] += n
        return first

    def remote(src, dst, device, slot):
        return pltpu.make_async_remote_copy(
            src_ref=src, dst_ref=dst, send_sem=s["send"].at[slot], recv_sem=s["recv"].at[slot],
            device_id=(device,), device_id_type=MESH)

    def push(src, dst, device):
        copy = remote(src, dst, device, sem())
        copy.start()
        sends.append(copy)
        return copy

    barrier = pltpu.get_barrier_semaphore()
    pl.semaphore_signal(barrier, inc=1, device_id=(partner,), device_id_type=MESH)
    for axis in (axis_p, axis_q, axis_z):
        for k in (1, 2, 3):
            pl.semaphore_signal(barrier, inc=1, device_id=(around(axis, k)[0],), device_id_type=MESH)

    dyf = dy_s[...].astype(F32)
    pdf = (po_s[...] * 16 + pl_s[...]).astype(F32)
    cols = jnp.transpose(jnp.concatenate(
        [jnp.exp(pred_s[...]), firm_s[...].astype(F32), dyf, pdf, jnp.zeros((64, 128), F32)], axis=0))
    lane = iota((128, 128), 1).astype(F32)
    for i in range(16):
        s["wc"][blk(i), :] = jnp.broadcast_to(cols[:, i:i + 1], (128, 128))
        s["fc"][blk(i), :] = (cols[:, 16 + i:17 + i] == lane).astype(F32).astype(BF16)
        s["dyc"][blk(i), :] = jnp.broadcast_to(cols[:, 32 + i:33 + i], (128, 128))
        s["pdc"][blk(i), :] = jnp.broadcast_to(cols[:, 48 + i:49 + i], (128, 128))

    @pl.loop(0, 4)
    def _(g):
        rows = pl.ds(pl.multiple_of(g * 512, 512), 512)
        hi, lo = split2(x_ref[rows, :] * s["wc"][rows, :])
        s["wv"][rows, 0:128] = hi
        s["wv"][rows, 128:256] = lo

    w_row = jnp.exp(pred_r[...])
    z_row = pred_r[...] + out_r[...] / w_row - 1.0
    wz_row = w_row * z_row
    firm_row = firm_r[...]
    sub = iota((128, 128), 0)
    acc_w = jnp.zeros((128, 128), F32)
    acc_z = jnp.zeros((128, 128), F32)
    for i in range(16):
        mask = jnp.broadcast_to(firm_row[:, blk(i)], (128, 128)) == sub
        s["ft"][:, blk(i)] = mask.astype(F32).astype(BF16)
        acc_w += jnp.where(mask, w_row[:, blk(i)], 0.0)
        acc_z += jnp.where(mask, wz_row[:, blk(i)], 0.0)
    firm_w = jnp.sum(acc_w, axis=1, keepdims=True)
    firm_z = jnp.sum(acc_z, axis=1, keepdims=True)
    den = jnp.where(firm_w > 0.0, firm_w, 1.0)
    firm_z = firm_z / den
    sums = dot(s["ft"][...], s["wv"][...])
    hi, lo = split2((sums[:, 0:128] + sums[:, 128:256]) / den)
    s["fm"][:, 0:128] = hi
    s["fm"][:, 128:256] = lo
    picks = []
    for i in range(16):
        mask = jnp.broadcast_to(firm_row[:, blk(i)], (128, 128)) == sub
        picks.append(jnp.sum(jnp.where(mask, firm_z, 0.0), axis=0, keepdims=True))
    z_row = z_row - jnp.concatenate(picks, axis=1)
    s["z"][...] = z_row
    wz_row = w_row * z_row

    @pl.loop(0, 4)
    def _(g):
        rows = pl.ds(pl.multiple_of(g * 512, 512), 512)
        got = dot(s["fc"][rows, :], s["fm"][...])
        v = x_ref[rows, :] - (got[:, 0:128] + got[:, 128:256])
        s["v"][rows, :] = v
        hi, lo = split2(v * s["wc"][rows, :])
        s["wv"][rows, 0:128] = hi
        s["wv"][rows, 128:256] = lo

    sub16 = iota((16, R), 0)

    def effects(own_row, loc_row, name):
        s[name + "_own"][...] = jnp.broadcast_to(own_row.astype(F32), (16, R)).astype(BF16)
        s[name + "_loc"][...] = (loc_row == sub16).astype(F32).astype(BF16)
        for i in range(16):
            s[name + "_ob"][:, blk(i)] = (
                jnp.broadcast_to(own_row[:, blk(i)], (128, 128)) == sub).astype(F32).astype(BF16)

    def table(name, slot):
        t_ref, got = s[name + "_t"], s[name + "_cr"]

        @pl.loop(0, 4)
        def _(it):
            base = lax.rem(theirs + it * 32, 128)
            for j in range(32):
                own = jnp.full((16, 128), 1.0, F32) * (base + j).astype(F32)
                own = jnp.concatenate([own.astype(BF16)] * 16, axis=1)
                s["lh"][blk(j, 16), :] = jnp.where(
                    s[name + "_own"][...] == own, s[name + "_loc"][...], jnp.zeros((16, R), BF16))
            sums = dot(s["lh"][...], s["wv"][...])
            t_ref[pl.ds(base, 32)] = (sums[:, 0:128] + sums[:, 128:256]).reshape(32, 16, 128)

            @pl.when(it < 2)
            def _():
                remote(t_ref.at[pl.ds(base, 32)], got.at[pl.ds(it * 32, 32)], partner, slot + it).start()

        for it in range(2):
            sends.append(remote(t_ref.at[pl.ds(theirs + it * 32, 32)], got.at[pl.ds(it * 32, 32)],
                                partner, slot + it))
        return sends[-2:]

    def scalar_sums(name, wz):
        hot = s[name + "_loc"][...].astype(F32)
        parts = []
        for row in (wz, w_row):
            for piece in split3(row):
                parts.append((hot * piece.astype(F32)).astype(BF16))
        e = dot_nt(jnp.concatenate(parts, axis=0), s[name + "_ob"][...])
        e = jnp.concatenate([e[0:16] + e[16:32] + e[32:48], e[48:64] + e[64:80] + e[80:96],
                             jnp.zeros((96, 128), F32)], axis=0)
        s[name + "_e"][...] = jnp.transpose(e).reshape(128, 1, 128)

    def rs_begin(name, axes):
        return {"n": name, "axes": axes, "live": None}

    def rs_send(job, stage):
        name, axis = job["n"], job["axes"][stage]
        part = (16, 4, 1)[stage]
        job["live"] = []
        for k in (1, 2, 3):
            device, j = around(axis, k)
            job["live"].append(push(s[f"{name}_a{stage}"].at[pl.ds(j * part, part)],
                                    s[f"{name}_r{stage}"].at[k - 1], device))

    def rs_wait(job, stage):
        name, (u, _) = job["n"], job["axes"][stage]
        part = (16, 4, 1)[stage]
        for copy in job["live"]:
            copy.wait_recv()
        got = s[f"{name}_r{stage}"]
        total = s[f"{name}_a{stage}"][pl.ds(u * part, part)] + got[0] + got[1] + got[2]
        if stage < 2:
            s[f"{name}_a{stage + 1}"][...] = total
        return total

    axes_dy = (axis_p, axis_q, axis_z)
    axes_pd = (axis_z, axis_p, axis_q)

    dy_row = dy_r[...]
    effects(lax.shift_right_logical(dy_row, 4), jnp.bitwise_and(dy_row, 15), "dy")
    pl.semaphore_wait(barrier, 10)
    dy_core = table("dy", sem(2))
    scalar_sums("dy", wz_row)
    dye_core = push(s["dy_e"].at[pl.ds(theirs, 64)], s["dy_ecr"], partner)
    for copy in dy_core:
        copy.wait_recv()
    s["dy_a0"][...] = s["dy_t"][pl.ds(mine, 64)] + s["dy_cr"][...]
    dy = rs_begin("dy", axes_dy)
    rs_send(dy, 0)
    dye_core.wait_recv()
    s["dye_a0"][...] = s["dy_e"][pl.ds(mine, 64)] + s["dy_ecr"][...]
    dye = rs_begin("dye", axes_dy)
    rs_send(dye, 0)

    po_row = po_r[...]
    pl_row = pl_r[...]
    effects(po_row, pl_row, "pd")
    upper = (iota((256, 256), 0) <= iota((256, 256), 1)).astype(F32).astype(BF16)
    carry = jnp.zeros((128, 1), F32)
    places = []
    for i in range(8):
        hot = s["pd_ob"][:, blk(i, 256)]
        run = dot(hot, upper) + carry
        carry = run[:, 255:256]
        places.append(jnp.sum(run * hot.astype(F32), axis=0, keepdims=True))
    place = jnp.concatenate(places, axis=1) - 1.0
    here = place == iota((32, R), 0).astype(F32)
    pieces = [lax.shift_right_logical(dy_row, 4).astype(F32), jnp.bitwise_and(dy_row, 15).astype(F32),
              pl_row.astype(F32)] + [v.astype(F32) for v in split3(w_row)]
    f = dot_nt(jnp.concatenate([jnp.where(here, v, 0.0).astype(BF16) for v in pieces], axis=0), s["pd_ob"][...])
    f = jnp.concatenate([f[0:32] * 16.0 + f[32:64], f[64:96], f[96:128] + f[128:160] + f[160:192],
                         jnp.zeros((32, 128), F32)], axis=0)
    s["f"][...] = jnp.transpose(f).reshape(128, 1, 128)
    f_live = [push(s["f"].at[pl.ds(theirs, 64)], s["f0"].at[1], partner)]
    s["f0"][0] = s["f"][pl.ds(mine, 64)]

    def f_send(stage):
        axis = axes_pd[stage]
        part = (16, 4, 1)[stage]
        src, dst = s[f"f{stage}"], s[f"f{stage + 1}"]
        pre = (slice(None),) * (stage + 1)
        f_live.clear()
        for k in (1, 2, 3):
            device, j = around(axis, k)
            f_live.append(push(src.at[pre + (pl.ds(j * part, part),)], dst.at[k], device))
        dst[0] = src[pre + (pl.ds(axis[0] * part, part),)]

    def f_wait():
        for copy in f_live:
            copy.wait_recv()

    pd_core = table("pd", sem(2))
    scalar_sums("pd", wz_row)
    pde_core = push(s["pd_e"].at[pl.ds(theirs, 64)], s["pd_ecr"], partner)

    rs_wait(dy, 0)
    rs_send(dy, 1)
    rs_wait(dye, 0)
    rs_send(dye, 1)
    for copy in pd_core:
        copy.wait_recv()
    s["pd_a0"][...] = s["pd_t"][pl.ds(mine, 64)] + s["pd_cr"][...]
    pd = rs_begin("pd", axes_pd)
    rs_send(pd, 0)
    pde_core.wait_recv()
    s["pde_a0"][...] = s["pd_e"][pl.ds(mine, 64)] + s["pd_ecr"][...]
    pde = rs_begin("pde", axes_pd)
    rs_send(pde, 0)
    f_wait()
    f_send(0)

    rs_wait(dy, 1)
    rs_send(dy, 2)
    rs_wait(dye, 1)
    rs_send(dye, 2)

    lane_id = iota((16, 128), 1)
    sub_id = iota((16, 128), 0)

    def column(e_row, first):
        spread = jnp.broadcast_to(e_row, (16, 128))
        return jnp.sum(jnp.where(lane_id == sub_id + first, spread, 0.0), axis=1, keepdims=True)

    def as_row(column16, first):
        spread = jnp.where(lane_id == sub_id + first, column16, 0.0)
        return jnp.sum(spread, axis=0, keepdims=True)

    def ag(name, block, row, order):
        full, fullz = s[name + "_m"], s[name + "_mz"]
        spots = {"p": p, "q": q, "z": z}
        own = [spots[a] for a in order]

        def view(fixed):
            index = [c] + [fixed[a] if a in fixed else slice(None) for a in order]
            return tuple(index)

        full[(c, *own)] = block
        fullz[(c, *own)] = row

        def stage(axis, fixed):
            out = []
            for k in (1, 2, 3):
                device, _ = around(axis, k)
                at = view(fixed)
                out.append((push(full.at[at], full.at[at], device), push(fullz.at[at], fullz.at[at], device)))
            return out

        def cross(fixed):
            at = view(fixed)
            return (push(full.at[at], full.at[at], partner), push(fullz.at[at], fullz.at[at], partner))

        def wait(copies):
            for pair in copies:
                for copy in pair:
                    copy.wait_recv()

        got = stage(axis_z, {"p": p, "q": q, "z": z})
        yield
        wait(got)
        got = stage(axis_q, {"p": p, "q": q})
        yield
        wait(got)
        got = stage(axis_p, {"p": p})
        last = [cross({"p": p})]
        yield
        for k in (1, 2, 3):
            wait([got[k - 1]])
            last.append(cross({"p": lax.rem(p + 4 - k, 4)}))
        yield
        wait(last)

    def onehot_cols(name):
        @pl.loop(0, 16)
        def _(i):
            rows = pl.ds(pl.multiple_of(i * 128, 128), 128)
            col = s[name + "c"][rows, :]
            for t in range(16):
                s[name + "_oh"][rows, blk(t)] = (col == lane + 128.0 * t).astype(F32).astype(BF16)

    onehot_cols("dy")

    block = rs_wait(dy, 2)[0]
    row = rs_wait(dye, 2)[0]
    w16 = column(row, 16)
    den = jnp.where(w16 > 0.0, w16, 1.0)
    lane_at = lax.rem(16 * c * 64 + 16 * (16 * p + 4 * q + z), 128)
    ag_dy = ag("dy", block / den, as_row(column(row, 0) / den, lane_at), ("p", "q", "z"))
    next(ag_dy)

    rs_wait(pd, 0)
    rs_send(pd, 1)
    rs_wait(pde, 0)
    rs_send(pde, 1)
    f_wait()
    f_send(1)
    next(ag_dy)
    onehot_cols("pd")
    next(ag_dy)
    rs_wait(pd, 1)
    rs_send(pd, 2)
    rs_wait(pde, 1)
    rs_send(pde, 2)
    f_wait()
    f_send(2)
    next(ag_dy)
    f_wait()

    rows_t = jnp.transpose(s["f3"][...].reshape(128, 128))
    dy_t = rows_t[0:32].astype(I32)
    high_t = lax.shift_right_logical(dy_t, 7) * 16 + rows_t[32:64].astype(I32)
    low_t = jnp.bitwise_and(dy_t, 127)
    w_hi, w_lo = split2(rows_t[64:96])
    w_hi, w_lo = w_hi.astype(F32), w_lo.astype(F32)
    sub256 = iota((256, 128), 0)
    pair = jnp.zeros((512, 128), F32)
    for g in range(4):
        for h in range(8):
            t = g * 8 + h
            there = jnp.broadcast_to(high_t[t:t + 1], (256, 128)) == sub256
            s["ml"][0:256, blk(h)] = jnp.where(there, w_hi[t:t + 1], 0.0).astype(BF16)
            s["ml"][256:512, blk(h)] = jnp.where(there, w_lo[t:t + 1], 0.0).astype(BF16)
            s["mr"][:, blk(h)] = (jnp.broadcast_to(low_t[t:t + 1], (128, 128)) == sub).astype(F32).astype(BF16)
        pair += dot_nt(s["ml"][...], s["mr"][...])
    pair = pair[0:256] + pair[256:512]
    p_hi, p_lo = split2(pair)
    m_lhs = jnp.concatenate(
        [jnp.concatenate([v[blk(a, 16)] for a in range(16)], axis=1) for v in (p_hi, p_lo)], axis=0)
    pd_block = rs_wait(pd, 2)[0]
    pd_row = rs_wait(pde, 2)[0]

    for _ in ag_dy:
        pass

    def halves(name):
        hi, lo = split2(s[name + "_m"][...].reshape(R, 128))
        s["mh"][:, 0:128] = hi
        s["mh"][:, 128:256] = lo
        return jnp.sum(s[name + "_mz"][...].reshape(16, 8, 128), axis=1)

    mz = halves("dy")
    mm = dot(m_lhs, s["mh"][...])
    mm = mm[0:16, 0:128] + mm[0:16, 128:256] + mm[16:32, 0:128]
    mmz = jnp.zeros((16, 128), F32)
    for a in range(16):
        mmz += pair[blk(a, 16)] * mz[a:a + 1]
    mmz = jnp.sum(mmz, axis=1, keepdims=True)
    w16 = column(pd_row, 16)
    den = jnp.where(w16 > 0.0, w16, 1.0)
    qx = (pd_block - mm) / den
    qz = (column(pd_row, 0) - mmz) / den
    lane_at = lax.rem(16 * c * 64 + 16 * (16 * z + 4 * p + q), 128)
    ag_pd = ag("pd", qx, as_row(qz, lane_at), ("z", "p", "q"))
    next(ag_pd)

    def pick(name, sink):
        @pl.loop(0, 4)
        def _(g):
            rows = pl.ds(pl.multiple_of(g * 512, 512), 512)
            got = dot(s[name + "_oh"][rows, :], s["mh"][...])
            sink[rows, :] = s["v"][rows, :] - (got[:, 0:128] + got[:, 128:256])

    def pick_z(index_row, mz):
        high = lax.shift_right_logical(index_row, 7)
        low = jnp.bitwise_and(index_row, 127)
        parts = jnp.concatenate([v.astype(F32) for v in split3(mz)], axis=0).astype(BF16)
        out = []
        for i in range(16):
            hot = (jnp.broadcast_to(low[:, blk(i)], (128, 128)) == sub).astype(F32).astype(BF16)
            got = dot(parts, hot)
            got = got[0:16] + got[16:32] + got[32:48]
            out.append(jnp.sum(jnp.where(high[:, blk(i)] == sub_id, got, 0.0), axis=0, keepdims=True))
        return jnp.concatenate(out, axis=1)

    pick("dy", s["v"])
    z_row = s["z"][...] - pick_z(dy_row, mz)
    next(ag_pd)

    for i in range(16):
        v = s["v"][blk(i), :]
        hi, lo = split2(v)
        s["vs"][blk(i), 0:128] = hi
        s["vs"][blk(i), 128:256] = lo
        hi, lo = split2(jnp.transpose(v * s["wc"][blk(i), :]))
        s["lg"][0:128, blk(i)] = hi
        s["lg"][128:256, blk(i)] = lo
    hi, lo = split2(w_row * z_row)
    row_id = iota((16, R), 0)
    s["lg"][256:272, :] = jnp.where(
        row_id == 0, hi.astype(F32), jnp.where(row_id == 1, lo.astype(F32), 0.0)).astype(BF16)
    g = dot(s["lg"][...], s["vs"][...])
    rhs_row = jnp.sum(g[256:272, 0:128] + g[256:272, 128:256], axis=0, keepdims=True)
    g = g[0:128, 0:128] + g[0:128, 128:256] + g[128:256, 0:128] + g[128:256, 128:256]
    wq = qx * w16
    g = g - lax.dot_general(wq, qx, (((0,), (0,)), ((), ())), precision=lax.Precision.HIGHEST,
                            preferred_element_type=F32)
    rhs_row = rhs_row - jnp.sum(wq * qz, axis=0, keepdims=True)
    eye = iota((128, 128), 0) == iota((128, 128), 1)
    rhs_col = jnp.sum(jnp.where(eye, rhs_row, 0.0), axis=1, keepdims=True)
    g = jnp.concatenate([g, jnp.broadcast_to(rhs_col, (128, 128))], axis=1)
    o = iota((128, 128), 0)
    oc, op = lax.shift_right_logical(o, 6), jnp.bitwise_and(lax.shift_right_logical(o, 4), 3)
    oq, oz = jnp.bitwise_and(lax.shift_right_logical(o, 2), 3), jnp.bitwise_and(o, 3)
    ox, oy = op + oc * (oq - op), oq + oc * (op - oq)
    order = (iota((128, 128), 1) == oz * 32 + ox * 8 + oy * 2 + oc).astype(F32).astype(BF16)
    s["g"][...] = sum(dot(order, v) for v in split3(g)).reshape(128, 1, 256)
    g_core = push(s["g"].at[pl.ds(theirs, 64)], s["g_cr"], partner)
    next(ag_pd)
    g_core.wait_recv()
    s["g_a0"][...] = s["g"][pl.ds(mine, 64)] + s["g_cr"][...]
    gram = rs_begin("g", axes_dy)
    rs_send(gram, 0)
    next(ag_pd)
    rs_wait(gram, 0)
    rs_send(gram, 1)
    for _ in ag_pd:
        pass
    mz = halves("pd")
    rs_wait(gram, 1)
    rs_send(gram, 2)
    pick("pd", xt_ref)
    zt_ref[...] = z_row - pick_z(po_row * 16 + pl_row, mz)
    g_row = rs_wait(gram, 2)[0] / total_rows
    gram_ref[...] = g_row[:, 0:128]
    rhs_ref[...] = g_row[:, 128:129]
    for copy in sends:
        copy.wait_send()


def scratch():
    v = pltpu.VMEM
    shapes = {
        "wc": v((R, 128), F32), "dyc": v((R, 128), F32), "pdc": v((R, 128), F32), "fc": v((R, 128), BF16),
        "ft": v((128, R), BF16), "fm": v((128, 256), BF16), "wv": v((R, 256), BF16), "v": v((R, 128), F32),
        "z": v((1, R), F32), "lh": v((512, R), BF16), "mh": v((R, 256), BF16),
        "dy_oh": v((R, 2048), BF16), "pd_oh": v((R, 2048), BF16),
        "ml": v((512, 1024), BF16), "mr": v((128, 1024), BF16), "vs": v((R, 256), BF16), "lg": v((272, R), BF16),
        "f": v((128, 1, 128), F32), "f0": v((2, 64, 1, 128), F32), "f1": v((4, 2, 16, 1, 128), F32),
        "f2": v((4, 4, 2, 4, 1, 128), F32), "f3": v((4, 4, 4, 2, 1, 1, 128), F32),
        "g": v((128, 1, 256), F32), "g_cr": v((64, 1, 256), F32),
    }
    for name in ("dy", "pd"):
        shapes[name + "_own"] = v((16, R), BF16)
        shapes[name + "_loc"] = v((16, R), BF16)
        shapes[name + "_ob"] = v((128, R), BF16)
        shapes[name + "_t"] = v((128, 16, 128), F32)
        shapes[name + "_cr"] = v((64, 16, 128), F32)
        shapes[name + "_e"] = v((128, 1, 128), F32)
        shapes[name + "_ecr"] = v((64, 1, 128), F32)
        shapes[name + "_m"] = v((2, 4, 4, 4, 16, 128), F32)
        shapes[name + "_mz"] = v((2, 4, 4, 4, 1, 128), F32)
    for name, tail in (("dy", (16, 128)), ("pd", (16, 128)), ("dye", (1, 128)), ("pde", (1, 128)), ("g", (1, 256))):
        for stage, part in enumerate((64, 16, 4)):
            shapes[f"{name}_a{stage}"] = v((part, *tail), F32)
            shapes[f"{name}_r{stage}"] = v((3, part // 4, *tail), F32)
    shapes["send"] = pltpu.SemaphoreType.DMA((160,))
    shapes["recv"] = pltpu.SemaphoreType.DMA((160,))
    return shapes


def shards(total_rows, covariates, outcome, predictor, firm_id, dy_id, pd_owner, pd_local):
    owner = pd_owner.reshape(R)
    rows = [v.reshape(1, R) for v in (outcome, predictor, firm_id, dy_id, owner, pd_local)]
    squares = [v.reshape(16, 128) for v in (predictor, firm_id, dy_id, owner, pd_local)]
    vmem = pl.BlockSpec(memory_space=pltpu.VMEM)
    xt, zt, gram, rhs = pl.pallas_call(
        functools.partial(kernel, total_rows),
        out_shape=(jax.ShapeDtypeStruct((R, 128), F32), jax.ShapeDtypeStruct((1, R), F32),
                   jax.ShapeDtypeStruct((1, 128), F32), jax.ShapeDtypeStruct((1, 1), F32)),
        in_specs=[vmem] * 12,
        out_specs=(vmem,) * 4,
        scratch_shapes=[scratch()],
        compiler_params=pltpu.CompilerParams(
            collective_id=0, has_side_effects=True, vmem_limit_bytes=63 * 1024 * 1024),
        name="demean",
    )(covariates, *rows, *squares)
    return xt, zt.reshape(R), gram, rhs.reshape(1)


def solution(mesh):
    specs = (P("rows", None), P("rows"), P("rows"), P("rows"), P("rows"), P("rows", None), P("rows"))
    out_specs = (P("rows", None), P("rows"), P("rows", None), P("rows"))
    return jax.shard_map(functools.partial(shards, float(R * 128)), mesh=mesh, in_specs=specs,
                         out_specs=out_specs, check_vma=False)
```

time: 633 us -> 77.7 us (0.12)
  the two profiles are of different devices: /device:TPU:1 before, /device:TPU:0 now
where the time goes in v1:
time: 77.7 us; the launch traced here: 77.5 us
  Pallas kernels  71.7 us (92%)
  local copies, waits for them, and re-layouts  3.39 us (4%)
  between operations  2.46 us (3%)
    pallas_call x1, Pallas kernels, shards(): pl.pallas_call(functools.partial(kernel, total_rows), out_shape=(jax.Shap...  71.7 us
    unnamed x7, local copies, waits for them, and re-layouts  3.39 us

profile of v1, /device:TPU:0, one launch (start us, length us, event | category | flops | bytes accessed | tf_op | source)
XLA Modules:
  0.0 77.5 jit_solution(15116054203229258435)
XLA Ops:
  0.6 71.7 %demean.1 = (f32[2048,128]{1,0:T(8,128)}, f32[1,2048]{1,0:T(1,128)}, f32[1,128]{1,0:T(1,128)}, f32[1,1]{1,0:T(1,128)}) custom-call(f32[2048,128]{1,0:T(8,128)} %x_ref.1, f32[1,2048]{1,0:T(1,128)} %bitcast.23, f32[1,2048]{1,0:T(1,128)} %bitcast.13, s32[1,2048]{1,0:T(1,128)} %bitcast.15, s32[1,2048]{1,0:T(1,128)} %bitcast.17, s32[1,2048]{1,0:T(1,128)} %bitcast.19, ...), custom_call_target="tpu_custom_call" | custom-call | tf_op jit(solution)/shard_map/demean/pallas_call | solution.py:544
  72.3 0.0 copy-start
  72.3 2.3 %copy.15 = f32[2048,128]{1,0:T(8,128)} copy(f32[2048,128]{1,0:T(8,128)} %get-tuple-element.16) | data formatting | bytes 2097152
  74.6 0.0 copy-done
  74.6 0.0 copy-start.1
  74.6 0.6 copy.16
  75.2 0.0 copy-done.1
  75.2 0.5 copy.17
Async XLA Ops:
  72.3 2.3 %copy-start = (f32[1,2048]{1,0:T(1,128)S(1)}, f32[1,2048]{1,0:T(1,128)}, u32[]{:S(2)}) copy-start(f32[1,2048]{1,0:T(1,128)} %get-tuple-element.9) | copy-start | bytes 24580
  74.6 0.6 copy-start.1

commit v2 on v1

--- a/solution.py
+++ b/solution.py
@@ -48,22 +48,19 @@
            xt_ref, zt_ref, gram_ref, rhs_ref, s):
     me = lax.axis_index("rows")
     c = lax.rem(me, 2)
-    y = lax.rem(lax.div(me, 2), 4)
-    x = lax.rem(lax.div(me, 8), 4)
-    z = lax.div(me, 32)
-    p = x + c * (y - x)
-    q = y + c * (x - y)
-    axis_p = (p, 8 - 6 * c)
-    axis_q = (q, 2 + 6 * c)
-    axis_z = (z, 32)
+    chip = lax.div(me, 2)
+    z, x, y = lax.div(chip, 16), lax.rem(lax.div(chip, 4), 4), lax.rem(chip, 4)
     partner = me + 1 - 2 * c
     mine = 64 * c
     theirs = 64 - mine
 
-    def around(axis, k):
-        u, stride = axis
-        j = lax.rem(u + k, 4)
-        return me + (j - u) * stride, j
+    def far(offset):
+        return sum(min(v, 4 - v) for v in offset)
+
+    offsets = sorted([(a, b, d) for a in range(4) for b in range(4) for d in range(4) if (a, b, d) != (0, 0, 0)],
+                     key=lambda v: -far(v))
+    chips = [(lax.rem(z + a, 4) * 16 + lax.rem(x + b, 4) * 4 + lax.rem(y + d, 4), a * 16 + b * 4 + d)
+             for a, b, d in offsets]
 
     counter = [0]
     sends = []
@@ -73,22 +70,49 @@
         counter[0] += n
         return first
 
-    def remote(src, dst, device, slot):
+    def remote(src, dst, device, send, recv):
         return pltpu.make_async_remote_copy(
-            src_ref=src, dst_ref=dst, send_sem=s["send"].at[slot], recv_sem=s["recv"].at[slot],
+            src_ref=src, dst_ref=dst, send_sem=s["send"].at[send], recv_sem=s["recv"].at[recv],
             device_id=(device,), device_id_type=MESH)
 
-    def push(src, dst, device):
-        copy = remote(src, dst, device, sem())
+    def wait_bytes(ref, which, slot):
+        pltpu.make_async_copy(ref, ref, s[which].at[slot]).wait()
+
+    def cross(src, dst):
+        slot = sem()
+        copy = remote(src, dst, partner, slot, slot)
         copy.start()
-        sends.append(copy)
-        return copy
+        sends.append(lambda: wait_bytes(src, "send", slot))
+        return lambda: wait_bytes(dst, "recv", slot)
+
+    def scatter(src, got):
+        slot = sem()
+        for j, offset in chips:
+            remote(src.at[j], got.at[offset], 2 * j + c, slot, slot).start()
+        got[0] = src[chip]
+        sends.append(lambda: wait_bytes(got.at[pl.ds(1, 63)], "send", slot))
+        return lambda: wait_bytes(got.at[pl.ds(1, 63)], "recv", slot)
+
+    def gather(full, block):
+        full[c, chip] = block
+        send, recv = sem(), sem(4)
+        for j, offset in chips:
+            remote(full.at[c, chip], full.at[c, chip], 2 * j + c, send, recv + offset // 16).start()
+        sends.append(lambda: wait_bytes(full.at[0, pl.ds(0, 63)], "send", send))
+        yield
+        waits = []
+        for step in (0, 1, 3, 2):
+            wait_bytes(full.at[0, pl.ds(0, 16 if step else 15)], "recv", recv + step)
+            plane = pl.ds(16 * lax.rem(z + 4 - step, 4), 16)
+            waits.append(cross(full.at[c, plane], full.at[c, plane]))
+        yield
+        for wait in waits:
+            wait()
 
     barrier = pltpu.get_barrier_semaphore()
     pl.semaphore_signal(barrier, inc=1, device_id=(partner,), device_id_type=MESH)
-    for axis in (axis_p, axis_q, axis_z):
-        for k in (1, 2, 3):
-            pl.semaphore_signal(barrier, inc=1, device_id=(around(axis, k)[0],), device_id_type=MESH)
+    for j, _ in chips:
+        pl.semaphore_signal(barrier, inc=1, device_id=(2 * j + c,), device_id_type=MESH)
 
     dyf = dy_s[...].astype(F32)
     pdf = (po_s[...] * 16 + pl_s[...]).astype(F32)
@@ -155,8 +179,9 @@
             s[name + "_ob"][:, blk(i)] = (
                 jnp.broadcast_to(own_row[:, blk(i)], (128, 128)) == sub).astype(F32).astype(BF16)
 
-    def table(name, slot):
+    def table(name):
         t_ref, got = s[name + "_t"], s[name + "_cr"]
+        slot = sem(2)
 
         @pl.loop(0, 4)
         def _(it):
@@ -167,16 +192,16 @@
                 s["lh"][blk(j, 16), :] = jnp.where(
                     s[name + "_own"][...] == own, s[name + "_loc"][...], jnp.zeros((16, R), BF16))
             sums = dot(s["lh"][...], s["wv"][...])
-            t_ref[pl.ds(base, 32)] = (sums[:, 0:128] + sums[:, 128:256]).reshape(32, 16, 128)
+            t_ref[pl.ds(base, 32), 0:16] = (sums[:, 0:128] + sums[:, 128:256]).reshape(32, 16, 128)
 
             @pl.when(it < 2)
             def _():
-                remote(t_ref.at[pl.ds(base, 32)], got.at[pl.ds(it * 32, 32)], partner, slot + it).start()
+                remote(t_ref.at[pl.ds(base, 32)], got.at[pl.ds(it * 32, 32)], partner, slot + it, slot + it).start()
 
         for it in range(2):
-            sends.append(remote(t_ref.at[pl.ds(theirs + it * 32, 32)], got.at[pl.ds(it * 32, 32)],
-                                partner, slot + it))
-        return sends[-2:]
+            sends.append(lambda it=it: wait_bytes(got.at[pl.ds(it * 32, 32)], "send", slot + it))
+        for it in range(2):
+            wait_bytes(got.at[pl.ds(it * 32, 32)], "recv", slot + it)
 
     def scalar_sums(name, wz):
         hot = s[name + "_loc"][...].astype(F32)
@@ -187,49 +212,15 @@
         e = dot_nt(jnp.concatenate(parts, axis=0), s[name + "_ob"][...])
         e = jnp.concatenate([e[0:16] + e[16:32] + e[32:48], e[48:64] + e[64:80] + e[80:96],
                              jnp.zeros((96, 128), F32)], axis=0)
-        s[name + "_e"][...] = jnp.transpose(e).reshape(128, 1, 128)
-
-    def rs_begin(name, axes):
-        return {"n": name, "axes": axes, "live": None}
-
-    def rs_send(job, stage):
-        name, axis = job["n"], job["axes"][stage]
-        part = (16, 4, 1)[stage]
-        job["live"] = []
-        for k in (1, 2, 3):
-            device, j = around(axis, k)
-            job["live"].append(push(s[f"{name}_a{stage}"].at[pl.ds(j * part, part)],
-                                    s[f"{name}_r{stage}"].at[k - 1], device))
-
-    def rs_wait(job, stage):
-        name, (u, _) = job["n"], job["axes"][stage]
-        part = (16, 4, 1)[stage]
-        for copy in job["live"]:
-            copy.wait_recv()
-        got = s[f"{name}_r{stage}"]
-        total = s[f"{name}_a{stage}"][pl.ds(u * part, part)] + got[0] + got[1] + got[2]
-        if stage < 2:
-            s[f"{name}_a{stage + 1}"][...] = total
-        return total
-
-    axes_dy = (axis_p, axis_q, axis_z)
-    axes_pd = (axis_z, axis_p, axis_q)
+        s[name + "_t"][:, 16:17] = jnp.transpose(e).reshape(128, 1, 128)
 
     dy_row = dy_r[...]
     effects(lax.shift_right_logical(dy_row, 4), jnp.bitwise_and(dy_row, 15), "dy")
-    pl.semaphore_wait(barrier, 10)
-    dy_core = table("dy", sem(2))
     scalar_sums("dy", wz_row)
-    dye_core = push(s["dy_e"].at[pl.ds(theirs, 64)], s["dy_ecr"], partner)
-    for copy in dy_core:
-        copy.wait_recv()
-    s["dy_a0"][...] = s["dy_t"][pl.ds(mine, 64)] + s["dy_cr"][...]
-    dy = rs_begin("dy", axes_dy)
-    rs_send(dy, 0)
-    dye_core.wait_recv()
-    s["dye_a0"][...] = s["dy_e"][pl.ds(mine, 64)] + s["dy_ecr"][...]
-    dye = rs_begin("dye", axes_dy)
-    rs_send(dye, 0)
+    pl.semaphore_wait(barrier, 64)
+    table("dy")
+    s["dy_a"][...] = s["dy_t"][pl.ds(mine, 64)] + s["dy_cr"][...]
+    dy_wait = scatter(s["dy_a"], s["dy_got"])
 
     po_row = po_r[...]
     pl_row = pl_r[...]
@@ -249,49 +240,13 @@
     f = dot_nt(jnp.concatenate([jnp.where(here, v, 0.0).astype(BF16) for v in pieces], axis=0), s["pd_ob"][...])
     f = jnp.concatenate([f[0:32] * 16.0 + f[32:64], f[64:96], f[96:128] + f[128:160] + f[160:192],
                          jnp.zeros((32, 128), F32)], axis=0)
-    s["f"][...] = jnp.transpose(f).reshape(128, 1, 128)
-    f_live = [push(s["f"].at[pl.ds(theirs, 64)], s["f0"].at[1], partner)]
-    s["f0"][0] = s["f"][pl.ds(mine, 64)]
-
-    def f_send(stage):
-        axis = axes_pd[stage]
-        part = (16, 4, 1)[stage]
-        src, dst = s[f"f{stage}"], s[f"f{stage + 1}"]
-        pre = (slice(None),) * (stage + 1)
-        f_live.clear()
-        for k in (1, 2, 3):
-            device, j = around(axis, k)
-            f_live.append(push(src.at[pre + (pl.ds(j * part, part),)], dst.at[k], device))
-        dst[0] = src[pre + (pl.ds(axis[0] * part, part),)]
-
-    def f_wait():
-        for copy in f_live:
-            copy.wait_recv()
-
-    pd_core = table("pd", sem(2))
+    s["pd_t"][:, 17:18] = jnp.transpose(f).reshape(128, 1, 128)
     scalar_sums("pd", wz_row)
-    pde_core = push(s["pd_e"].at[pl.ds(theirs, 64)], s["pd_ecr"], partner)
-
-    rs_wait(dy, 0)
-    rs_send(dy, 1)
-    rs_wait(dye, 0)
-    rs_send(dye, 1)
-    for copy in pd_core:
-        copy.wait_recv()
-    s["pd_a0"][...] = s["pd_t"][pl.ds(mine, 64)] + s["pd_cr"][...]
-    pd = rs_begin("pd", axes_pd)
-    rs_send(pd, 0)
-    pde_core.wait_recv()
-    s["pde_a0"][...] = s["pd_e"][pl.ds(mine, 64)] + s["pd_ecr"][...]
-    pde = rs_begin("pde", axes_pd)
-    rs_send(pde, 0)
-    f_wait()
-    f_send(0)
-
-    rs_wait(dy, 1)
-    rs_send(dy, 2)
-    rs_wait(dye, 1)
-    rs_send(dye, 2)
+    table("pd")
+    s["pd_a"][:, 0:17] = s["pd_t"][pl.ds(mine, 64), 0:17] + s["pd_cr"][:, 0:17]
+    s["pd_a"][:, 17:18] = s["pd_t"][pl.ds(mine, 64), 17:18]
+    s["pd_a"][:, 18:19] = s["pd_cr"][:, 17:18]
+    pd_wait = scatter(s["pd_a"], s["pd_got"])
 
     lane_id = iota((16, 128), 1)
     sub_id = iota((16, 128), 0)
@@ -303,50 +258,6 @@
     def as_row(column16, first):
         spread = jnp.where(lane_id == sub_id + first, column16, 0.0)
         return jnp.sum(spread, axis=0, keepdims=True)
-
-    def ag(name, block, row, order):
-        full, fullz = s[name + "_m"], s[name + "_mz"]
-        spots = {"p": p, "q": q, "z": z}
-        own = [spots[a] for a in order]
-
-        def view(fixed):
-            index = [c] + [fixed[a] if a in fixed else slice(None) for a in order]
-            return tuple(index)
-
-        full[(c, *own)] = block
-        fullz[(c, *own)] = row
-
-        def stage(axis, fixed):
-            out = []
-            for k in (1, 2, 3):
-                device, _ = around(axis, k)
-                at = view(fixed)
-                out.append((push(full.at[at], full.at[at], device), push(fullz.at[at], fullz.at[at], device)))
-            return out
-
-        def cross(fixed):
-            at = view(fixed)
-            return (push(full.at[at], full.at[at], partner), push(fullz.at[at], fullz.at[at], partner))
-
-        def wait(copies):
-            for pair in copies:
-                for copy in pair:
-                    copy.wait_recv()
-
-        got = stage(axis_z, {"p": p, "q": q, "z": z})
-        yield
-        wait(got)
-        got = stage(axis_q, {"p": p, "q": q})
-        yield
-        wait(got)
-        got = stage(axis_p, {"p": p})
-        last = [cross({"p": p})]
-        yield
-        for k in (1, 2, 3):
-            wait([got[k - 1]])
-            last.append(cross({"p": lax.rem(p + 4 - k, 4)}))
-        yield
-        wait(last)
 
     def onehot_cols(name):
         @pl.loop(0, 16)
@@ -357,34 +268,18 @@
                 s[name + "_oh"][rows, blk(t)] = (col == lane + 128.0 * t).astype(F32).astype(BF16)
 
     onehot_cols("dy")
-
-    block = rs_wait(dy, 2)[0]
-    row = rs_wait(dye, 2)[0]
+    dy_wait()
+    total = jnp.sum(s["dy_got"][...], axis=0)
+    row = total[16:17]
     w16 = column(row, 16)
     den = jnp.where(w16 > 0.0, w16, 1.0)
-    lane_at = lax.rem(16 * c * 64 + 16 * (16 * p + 4 * q + z), 128)
-    ag_dy = ag("dy", block / den, as_row(column(row, 0) / den, lane_at), ("p", "q", "z"))
-    next(ag_dy)
-
-    rs_wait(pd, 0)
-    rs_send(pd, 1)
-    rs_wait(pde, 0)
-    rs_send(pde, 1)
-    f_wait()
-    f_send(1)
+    lane_at = 16 * lax.rem(chip, 8)
+    ag_dy = gather(s["dy_m"], jnp.concatenate([total[0:16] / den, as_row(column(row, 0) / den, lane_at)], axis=0))
     next(ag_dy)
     onehot_cols("pd")
-    next(ag_dy)
-    rs_wait(pd, 1)
-    rs_send(pd, 2)
-    rs_wait(pde, 1)
-    rs_send(pde, 2)
-    f_wait()
-    f_send(2)
-    next(ag_dy)
-    f_wait()
-
-    rows_t = jnp.transpose(s["f3"][...].reshape(128, 128))
+    pd_wait()
+
+    rows_t = jnp.transpose(s["pd_got"][:, 17:19].reshape(128, 128))
     dy_t = rows_t[0:32].astype(I32)
     high_t = lax.shift_right_logical(dy_t, 7) * 16 + rows_t[32:64].astype(I32)
     low_t = jnp.bitwise_and(dy_t, 127)
@@ -404,17 +299,17 @@
     p_hi, p_lo = split2(pair)
     m_lhs = jnp.concatenate(
         [jnp.concatenate([v[blk(a, 16)] for a in range(16)], axis=1) for v in (p_hi, p_lo)], axis=0)
-    pd_block = rs_wait(pd, 2)[0]
-    pd_row = rs_wait(pde, 2)[0]
+    pd_total = jnp.sum(s["pd_got"][:, 0:17], axis=0)
+    pd_block, pd_row = pd_total[0:16], pd_total[16:17]
 
     for _ in ag_dy:
         pass
 
     def halves(name):
-        hi, lo = split2(s[name + "_m"][...].reshape(R, 128))
+        hi, lo = split2(s[name + "_m"][:, :, 0:16].reshape(R, 128))
         s["mh"][:, 0:128] = hi
         s["mh"][:, 128:256] = lo
-        return jnp.sum(s[name + "_mz"][...].reshape(16, 8, 128), axis=1)
+        return jnp.sum(s[name + "_m"][:, :, 16:17].reshape(16, 8, 128), axis=1)
 
     mz = halves("dy")
     mm = dot(m_lhs, s["mh"][...])
@@ -427,8 +322,7 @@
     den = jnp.where(w16 > 0.0, w16, 1.0)
     qx = (pd_block - mm) / den
     qz = (column(pd_row, 0) - mmz) / den
-    lane_at = lax.rem(16 * c * 64 + 16 * (16 * z + 4 * p + q), 128)
-    ag_pd = ag("pd", qx, as_row(qz, lane_at), ("z", "p", "q"))
+    ag_pd = gather(s["pd_m"], jnp.concatenate([qx, as_row(qz, lane_at)], axis=0))
     next(ag_pd)
 
     def pick(name, sink):
@@ -452,7 +346,6 @@
 
     pick("dy", s["v"])
     z_row = s["z"][...] - pick_z(dy_row, mz)
-    next(ag_pd)
 
     for i in range(16):
         v = s["v"][blk(i), :]
@@ -477,32 +370,24 @@
     rhs_col = jnp.sum(jnp.where(eye, rhs_row, 0.0), axis=1, keepdims=True)
     g = jnp.concatenate([g, jnp.broadcast_to(rhs_col, (128, 128))], axis=1)
     o = iota((128, 128), 0)
-    oc, op = lax.shift_right_logical(o, 6), jnp.bitwise_and(lax.shift_right_logical(o, 4), 3)
-    oq, oz = jnp.bitwise_and(lax.shift_right_logical(o, 2), 3), jnp.bitwise_and(o, 3)
-    ox, oy = op + oc * (oq - op), oq + oc * (op - oq)
-    order = (iota((128, 128), 1) == oz * 32 + ox * 8 + oy * 2 + oc).astype(F32).astype(BF16)
+    device = 2 * jnp.bitwise_and(o, 63) + lax.shift_right_logical(o, 6)
+    order = (iota((128, 128), 1) == device).astype(F32).astype(BF16)
     s["g"][...] = sum(dot(order, v) for v in split3(g)).reshape(128, 1, 256)
-    g_core = push(s["g"].at[pl.ds(theirs, 64)], s["g_cr"], partner)
-    next(ag_pd)
-    g_core.wait_recv()
-    s["g_a0"][...] = s["g"][pl.ds(mine, 64)] + s["g_cr"][...]
-    gram = rs_begin("g", axes_dy)
-    rs_send(gram, 0)
-    next(ag_pd)
-    rs_wait(gram, 0)
-    rs_send(gram, 1)
+    g_wait = cross(s["g"].at[pl.ds(theirs, 64)], s["g_cr"])
+    g_wait()
+    s["g_a"][...] = s["g"][pl.ds(mine, 64)] + s["g_cr"][...]
+    g_wait = scatter(s["g_a"], s["g_got"])
     for _ in ag_pd:
         pass
     mz = halves("pd")
-    rs_wait(gram, 1)
-    rs_send(gram, 2)
     pick("pd", xt_ref)
     zt_ref[...] = z_row - pick_z(po_row * 16 + pl_row, mz)
-    g_row = rs_wait(gram, 2)[0] / total_rows
+    g_wait()
+    g_row = jnp.sum(s["g_got"][...], axis=0) / total_rows
     gram_ref[...] = g_row[:, 0:128]
     rhs_ref[...] = g_row[:, 128:129]
-    for copy in sends:
-        copy.wait_send()
+    for wait in sends:
+        wait()
 
 
 def scratch():
@@ -513,26 +398,21 @@
         "z": v((1, R), F32), "lh": v((512, R), BF16), "mh": v((R, 256), BF16),
         "dy_oh": v((R, 2048), BF16), "pd_oh": v((R, 2048), BF16),
         "ml": v((512, 1024), BF16), "mr": v((128, 1024), BF16), "vs": v((R, 256), BF16), "lg": v((272, R), BF16),
-        "f": v((128, 1, 128), F32), "f0": v((2, 64, 1, 128), F32), "f1": v((4, 2, 16, 1, 128), F32),
-        "f2": v((4, 4, 2, 4, 1, 128), F32), "f3": v((4, 4, 4, 2, 1, 1, 128), F32),
-        "g": v((128, 1, 256), F32), "g_cr": v((64, 1, 256), F32),
+        "g": v((128, 1, 256), F32), "g_cr": v((64, 1, 256), F32), "g_a": v((64, 1, 256), F32),
+        "g_got": v((64, 1, 256), F32),
     }
-    for name in ("dy", "pd"):
+    for name, extra in (("dy", 1), ("pd", 3)):
+        sent = 16 + min(extra, 2)
         shapes[name + "_own"] = v((16, R), BF16)
         shapes[name + "_loc"] = v((16, R), BF16)
         shapes[name + "_ob"] = v((128, R), BF16)
-        shapes[name + "_t"] = v((128, 16, 128), F32)
-        shapes[name + "_cr"] = v((64, 16, 128), F32)
-        shapes[name + "_e"] = v((128, 1, 128), F32)
-        shapes[name + "_ecr"] = v((64, 1, 128), F32)
-        shapes[name + "_m"] = v((2, 4, 4, 4, 16, 128), F32)
-        shapes[name + "_mz"] = v((2, 4, 4, 4, 1, 128), F32)
-    for name, tail in (("dy", (16, 128)), ("pd", (16, 128)), ("dye", (1, 128)), ("pde", (1, 128)), ("g", (1, 256))):
-        for stage, part in enumerate((64, 16, 4)):
-            shapes[f"{name}_a{stage}"] = v((part, *tail), F32)
-            shapes[f"{name}_r{stage}"] = v((3, part // 4, *tail), F32)
-    shapes["send"] = pltpu.SemaphoreType.DMA((160,))
-    shapes["recv"] = pltpu.SemaphoreType.DMA((160,))
+        shapes[name + "_t"] = v((128, sent, 128), F32)
+        shapes[name + "_cr"] = v((64, sent, 128), F32)
+        shapes[name + "_a"] = v((64, 16 + extra, 128), F32)
+        shapes[name + "_got"] = v((64, 16 + extra, 128), F32)
+        shapes[name + "_m"] = v((2, 64, 17, 128), F32)
+    shapes["send"] = pltpu.SemaphoreType.DMA((32,))
+    shapes["recv"] = pltpu.SemaphoreType.DMA((32,))
     return shapes
 
 

time: 77.7 us -> 61.5 us (0.79)
  the two profiles are of different devices: /device:TPU:0 before, /device:TPU:1 now
where the time goes in v2:
time: 61.5 us; the launch traced here: 61.3 us
  Pallas kernels  55.4 us (90%)
  local copies, waits for them, and re-layouts  3.39 us (6%)
  between operations  2.46 us (4%)
    pallas_call x1, Pallas kernels, shards(): pl.pallas_call(functools.partial(kernel, total_rows), out_shape=(jax.Shap...  55.4 us
    unnamed x7, local copies, waits for them, and re-layouts  3.39 us

profile of v2, /device:TPU:1, one launch (start us, length us, event | category | flops | bytes accessed | tf_op | source)
XLA Modules:
  0.0 61.3 jit_solution(4879748705157561193)
XLA Ops:
  0.6 55.4 %demean.1 = (f32[2048,128]{1,0:T(8,128)}, f32[1,2048]{1,0:T(1,128)}, f32[1,128]{1,0:T(1,128)}, f32[1,1]{1,0:T(1,128)}) custom-call(f32[2048,128]{1,0:T(8,128)} %x_ref.1, f32[1,2048]{1,0:T(1,128)} %bitcast.23, f32[1,2048]{1,0:T(1,128)} %bitcast.13, s32[1,2048]{1,0:T(1,128)} %bitcast.15, s32[1,2048]{1,0:T(1,128)} %bitcast.17, s32[1,2048]{1,0:T(1,128)} %bitcast.19, ...), custom_call_target="tpu_custom_call" | custom-call | tf_op jit(solution)/shard_map/demean/pallas_call | solution.py:424
  56.1 0.0 copy-start
  56.1 2.3 %copy.15 = f32[2048,128]{1,0:T(8,128)} copy(f32[2048,128]{1,0:T(8,128)} %get-tuple-element.16) | data formatting | bytes 2097152
  58.4 0.0 copy-done
  58.4 0.0 copy-start.1
  58.4 0.6 copy.16
  59.0 0.0 copy-done.1
  59.0 0.5 copy.17
Async XLA Ops:
  56.1 2.3 %copy-start = (f32[1,2048]{1,0:T(1,128)S(1)}, f32[1,2048]{1,0:T(1,128)}, u32[]{:S(2)}) copy-start(f32[1,2048]{1,0:T(1,128)} %get-tuple-element.9) | copy-start | bytes 24580
  58.4 0.6 copy-start.1

commit v3 on v2

--- a/solution.py
+++ b/solution.py
@@ -48,8 +48,10 @@
            xt_ref, zt_ref, gram_ref, rhs_ref, s):
     me = lax.axis_index("rows")
     c = lax.rem(me, 2)
-    chip = lax.div(me, 2)
-    z, x, y = lax.div(chip, 16), lax.rem(lax.div(chip, 4), 4), lax.rem(chip, 4)
+    y, x, z = lax.rem(lax.div(me, 2), 4), lax.rem(lax.div(me, 8), 4), lax.div(me, 32)
+    p = x + c * (y - x)
+    q = y + c * (x - y)
+    place = p * 16 + q * 4 + z
     partner = me + 1 - 2 * c
     mine = 64 * c
     theirs = 64 - mine
@@ -57,10 +59,13 @@
     def far(offset):
         return sum(min(v, 4 - v) for v in offset)
 
+    def at(a, b, d):
+        pp, qq, zz = lax.rem(p + a, 4), lax.rem(q + b, 4), lax.rem(z + d, 4)
+        return pp * 16 + qq * 4 + zz, c + pp * (8 - 6 * c) + qq * (2 + 6 * c) + zz * 32
+
     offsets = sorted([(a, b, d) for a in range(4) for b in range(4) for d in range(4) if (a, b, d) != (0, 0, 0)],
                      key=lambda v: -far(v))
-    chips = [(lax.rem(z + a, 4) * 16 + lax.rem(x + b, 4) * 4 + lax.rem(y + d, 4), a * 16 + b * 4 + d)
-             for a, b, d in offsets]
+    chips = [(*at(*v), v[0] * 16 + v[1] * 4 + v[2]) for v in offsets]
 
     counter = [0]
     sends = []
@@ -87,32 +92,52 @@
 
     def scatter(src, got):
         slot = sem()
-        for j, offset in chips:
-            remote(src.at[j], got.at[offset], 2 * j + c, slot, slot).start()
-        got[0] = src[chip]
+        for j, device, offset in chips:
+            remote(src.at[j], got.at[offset], device, slot, slot).start()
+        got[0] = src[place]
         sends.append(lambda: wait_bytes(got.at[pl.ds(1, 63)], "send", slot))
         return lambda: wait_bytes(got.at[pl.ds(1, 63)], "recv", slot)
 
+    def scatter_first(src, got):
+        slot = sem()
+        for k in (2, 1, 3):
+            _, device = at(k, 0, 0)
+            remote(src.at[pl.ds(16 * lax.rem(p + k, 4), 16)], got.at[k - 1], device, slot, slot).start()
+        sends.append(lambda: wait_bytes(got, "send", slot))
+        return lambda: wait_bytes(got, "recv", slot)
+
+    def scatter_rest(src, got):
+        slot = sem()
+        plane = [v for v in offsets if v[0] == 0]
+        for v in plane:
+            j, device = at(*v)
+            remote(src.at[lax.rem(j, 16)], got.at[v[1] * 4 + v[2]], device, slot, slot).start()
+        got[0] = src[lax.rem(place, 16)]
+        sends.append(lambda: wait_bytes(got.at[pl.ds(1, 15)], "send", slot))
+        return lambda: wait_bytes(got.at[pl.ds(1, 15)], "recv", slot)
+
     def gather(full, block):
-        full[c, chip] = block
+        full[c, place] = block
         send, recv = sem(), sem(4)
-        for j, offset in chips:
-            remote(full.at[c, chip], full.at[c, chip], 2 * j + c, send, recv + offset // 16).start()
+        for _, device, offset in chips:
+            remote(full.at[c, place], full.at[c, place], device, send, recv + offset // 16).start()
         sends.append(lambda: wait_bytes(full.at[0, pl.ds(0, 63)], "send", send))
-        yield
+        yield None
         waits = []
         for step in (0, 1, 3, 2):
             wait_bytes(full.at[0, pl.ds(0, 16 if step else 15)], "recv", recv + step)
-            plane = pl.ds(16 * lax.rem(z + 4 - step, 4), 16)
+            first = lax.rem(p + 4 - step, 4)
+            plane = pl.ds(16 * first, 16)
             waits.append(cross(full.at[c, plane], full.at[c, plane]))
-        yield
-        for wait in waits:
+            yield c, first
+        for step, wait in zip((0, 1, 3, 2), waits):
             wait()
+            yield 1 - c, lax.rem(q + 4 - step, 4)
 
     barrier = pltpu.get_barrier_semaphore()
     pl.semaphore_signal(barrier, inc=1, device_id=(partner,), device_id_type=MESH)
-    for j, _ in chips:
-        pl.semaphore_signal(barrier, inc=1, device_id=(2 * j + c,), device_id_type=MESH)
+    for _, device, _ in chips:
+        pl.semaphore_signal(barrier, inc=1, device_id=(device,), device_id_type=MESH)
 
     dyf = dy_s[...].astype(F32)
     pdf = (po_s[...] * 16 + pl_s[...]).astype(F32)
@@ -233,20 +258,22 @@
         run = dot(hot, upper) + carry
         carry = run[:, 255:256]
         places.append(jnp.sum(run * hot.astype(F32), axis=0, keepdims=True))
-    place = jnp.concatenate(places, axis=1) - 1.0
-    here = place == iota((32, R), 0).astype(F32)
+    here = jnp.concatenate(places, axis=1) - 1.0 == iota((32, R), 0).astype(F32)
     pieces = [lax.shift_right_logical(dy_row, 4).astype(F32), jnp.bitwise_and(dy_row, 15).astype(F32),
               pl_row.astype(F32)] + [v.astype(F32) for v in split3(w_row)]
     f = dot_nt(jnp.concatenate([jnp.where(here, v, 0.0).astype(BF16) for v in pieces], axis=0), s["pd_ob"][...])
     f = jnp.concatenate([f[0:32] * 16.0 + f[32:64], f[64:96], f[96:128] + f[128:160] + f[160:192],
                          jnp.zeros((32, 128), F32)], axis=0)
-    s["pd_t"][:, 17:18] = jnp.transpose(f).reshape(128, 1, 128)
+    s["f"][...] = jnp.transpose(f).reshape(128, 1, 128)
+    f_wait = cross(s["f"].at[pl.ds(theirs, 64)], s["f_cr"])
     scalar_sums("pd", wz_row)
     table("pd")
-    s["pd_a"][:, 0:17] = s["pd_t"][pl.ds(mine, 64), 0:17] + s["pd_cr"][:, 0:17]
-    s["pd_a"][:, 17:18] = s["pd_t"][pl.ds(mine, 64), 17:18]
-    s["pd_a"][:, 18:19] = s["pd_cr"][:, 17:18]
-    pd_wait = scatter(s["pd_a"], s["pd_got"])
+    f_wait()
+    s["f_a"][:, 0:1] = s["f"][pl.ds(mine, 64)]
+    s["f_a"][:, 1:2] = s["f_cr"][...]
+    f_wait = scatter(s["f_a"], s["f_got"])
+    s["pd_a"][...] = s["pd_t"][pl.ds(mine, 64)] + s["pd_cr"][...]
+    pd_wait = scatter_first(s["pd_a"], s["pd_first"])
 
     lane_id = iota((16, 128), 1)
     sub_id = iota((16, 128), 0)
@@ -265,7 +292,7 @@
             rows = pl.ds(pl.multiple_of(i * 128, 128), 128)
             col = s[name + "c"][rows, :]
             for t in range(16):
-                s[name + "_oh"][rows, blk(t)] = (col == lane + 128.0 * t).astype(F32).astype(BF16)
+                s[name + "_oh"][t // 2, rows, blk(t % 2)] = (col == lane + 128.0 * t).astype(F32).astype(BF16)
 
     onehot_cols("dy")
     dy_wait()
@@ -273,13 +300,13 @@
     row = total[16:17]
     w16 = column(row, 16)
     den = jnp.where(w16 > 0.0, w16, 1.0)
-    lane_at = 16 * lax.rem(chip, 8)
+    lane_at = 16 * lax.rem(place, 8)
     ag_dy = gather(s["dy_m"], jnp.concatenate([total[0:16] / den, as_row(column(row, 0) / den, lane_at)], axis=0))
     next(ag_dy)
     onehot_cols("pd")
-    pd_wait()
-
-    rows_t = jnp.transpose(s["pd_got"][:, 17:19].reshape(128, 128))
+    f_wait()
+
+    rows_t = jnp.transpose(s["f_got"][...].reshape(128, 128))
     dy_t = rows_t[0:32].astype(I32)
     high_t = lax.shift_right_logical(dy_t, 7) * 16 + rows_t[32:64].astype(I32)
     low_t = jnp.bitwise_and(dy_t, 127)
@@ -297,40 +324,53 @@
         pair += dot_nt(s["ml"][...], s["mr"][...])
     pair = pair[0:256] + pair[256:512]
     p_hi, p_lo = split2(pair)
-    m_lhs = jnp.concatenate(
-        [jnp.concatenate([v[blk(a, 16)] for a in range(16)], axis=1) for v in (p_hi, p_lo)], axis=0)
-    pd_total = jnp.sum(s["pd_got"][:, 0:17], axis=0)
-    pd_block, pd_row = pd_total[0:16], pd_total[16:17]
-
-    for _ in ag_dy:
-        pass
-
-    def halves(name):
-        hi, lo = split2(s[name + "_m"][:, :, 0:16].reshape(R, 128))
-        s["mh"][:, 0:128] = hi
-        s["mh"][:, 128:256] = lo
-        return jnp.sum(s[name + "_m"][:, :, 16:17].reshape(16, 8, 128), axis=1)
-
-    mz = halves("dy")
-    mm = dot(m_lhs, s["mh"][...])
-    mm = mm[0:16, 0:128] + mm[0:16, 128:256] + mm[16:32, 0:128]
+    for k in range(8):
+        s["mm"][k] = jnp.concatenate([jnp.concatenate([v[blk(2 * k, 16)], v[blk(2 * k + 1, 16)]], axis=1)
+                                      for v in (p_hi, p_lo)], axis=0)
+    pd_wait()
+    part = pl.ds(16 * p, 16)
+    s["pd_b"][...] = s["pd_a"][part] + s["pd_first"][0] + s["pd_first"][1] + s["pd_first"][2]
+    pd_wait = scatter_rest(s["pd_b"], s["pd_got"])
+
+    def plane_halves(name, half, first):
+        k = 4 * half + first
+        rows = pl.ds(pl.multiple_of(256 * k, 256), 256)
+        owners = pl.ds(16 * first, 16)
+        hi, lo = split2(s[name + "_m"][half, owners, 0:16].reshape(256, 128))
+        s["mh"][rows, 0:128] = hi
+        s["mh"][rows, 128:256] = lo
+        s[name + "_mz"][k] = jnp.sum(s[name + "_m"][half, owners, 16:17].reshape(2, 8, 128), axis=1)
+        return k, rows
+
+    acc = jnp.zeros((32, 256), F32)
+    for half, first in ag_dy:
+        k, rows = plane_halves("dy", half, first)
+        acc += dot(s["mm"][k], s["mh"][rows, :])
+    mm = acc[0:16, 0:128] + acc[0:16, 128:256] + acc[16:32, 0:128]
+    mz = s["dy_mz"][...].reshape(16, 128)
     mmz = jnp.zeros((16, 128), F32)
     for a in range(16):
         mmz += pair[blk(a, 16)] * mz[a:a + 1]
     mmz = jnp.sum(mmz, axis=1, keepdims=True)
+    pd_wait()
+    pd_total = jnp.sum(s["pd_got"][...], axis=0)
+    pd_row = pd_total[16:17]
     w16 = column(pd_row, 16)
     den = jnp.where(w16 > 0.0, w16, 1.0)
-    qx = (pd_block - mm) / den
+    qx = (pd_total[0:16] - mm) / den
     qz = (column(pd_row, 0) - mmz) / den
     ag_pd = gather(s["pd_m"], jnp.concatenate([qx, as_row(qz, lane_at)], axis=0))
     next(ag_pd)
 
-    def pick(name, sink):
-        @pl.loop(0, 4)
-        def _(g):
-            rows = pl.ds(pl.multiple_of(g * 512, 512), 512)
-            got = dot(s[name + "_oh"][rows, :], s["mh"][...])
-            sink[rows, :] = s["v"][rows, :] - (got[:, 0:128] + got[:, 128:256])
+    @pl.loop(0, 4)
+    def _(g):
+        rows = pl.ds(pl.multiple_of(g * 512, 512), 512)
+        got = jnp.zeros((512, 256), F32)
+        for k in range(8):
+            got += dot(s["dy_oh"][k, rows, :], s["mh"][blk(k, 256), :])
+        v = s["v"][rows, :] - (got[:, 0:128] + got[:, 128:256])
+        s["v"][rows, :] = v
+        xt_ref[rows, :] = v
 
     def pick_z(index_row, mz):
         high = lax.shift_right_logical(index_row, 7)
@@ -344,7 +384,6 @@
             out.append(jnp.sum(jnp.where(high[:, blk(i)] == sub_id, got, 0.0), axis=0, keepdims=True))
         return jnp.concatenate(out, axis=1)
 
-    pick("dy", s["v"])
     z_row = s["z"][...] - pick_z(dy_row, mz)
 
     for i in range(16):
@@ -370,18 +409,25 @@
     rhs_col = jnp.sum(jnp.where(eye, rhs_row, 0.0), axis=1, keepdims=True)
     g = jnp.concatenate([g, jnp.broadcast_to(rhs_col, (128, 128))], axis=1)
     o = iota((128, 128), 0)
-    device = 2 * jnp.bitwise_and(o, 63) + lax.shift_right_logical(o, 6)
+    oc, op = lax.shift_right_logical(o, 6), jnp.bitwise_and(lax.shift_right_logical(o, 4), 3)
+    oq, oz = jnp.bitwise_and(lax.shift_right_logical(o, 2), 3), jnp.bitwise_and(o, 3)
+    device = oc + op * (8 - 6 * oc) + oq * (2 + 6 * oc) + oz * 32
     order = (iota((128, 128), 1) == device).astype(F32).astype(BF16)
     s["g"][...] = sum(dot(order, v) for v in split3(g)).reshape(128, 1, 256)
     g_wait = cross(s["g"].at[pl.ds(theirs, 64)], s["g_cr"])
     g_wait()
     s["g_a"][...] = s["g"][pl.ds(mine, 64)] + s["g_cr"][...]
     g_wait = scatter(s["g_a"], s["g_got"])
-    for _ in ag_pd:
-        pass
-    mz = halves("pd")
-    pick("pd", xt_ref)
-    zt_ref[...] = z_row - pick_z(po_row * 16 + pl_row, mz)
+    for half, first in ag_pd:
+        k, part = plane_halves("pd", half, first)
+
+        @pl.loop(0, 4)
+        def _(g):
+            rows = pl.ds(pl.multiple_of(g * 512, 512), 512)
+            got = dot(s["pd_oh"][k, rows, :], s["mh"][part, :])
+            xt_ref[rows, :] -= got[:, 0:128] + got[:, 128:256]
+
+    zt_ref[...] = z_row - pick_z(po_row * 16 + pl_row, s["pd_mz"][...].reshape(16, 128))
     g_wait()
     g_row = jnp.sum(s["g_got"][...], axis=0) / total_rows
     gram_ref[...] = g_row[:, 0:128]
@@ -396,21 +442,23 @@
         "wc": v((R, 128), F32), "dyc": v((R, 128), F32), "pdc": v((R, 128), F32), "fc": v((R, 128), BF16),
         "ft": v((128, R), BF16), "fm": v((128, 256), BF16), "wv": v((R, 256), BF16), "v": v((R, 128), F32),
         "z": v((1, R), F32), "lh": v((512, R), BF16), "mh": v((R, 256), BF16),
-        "dy_oh": v((R, 2048), BF16), "pd_oh": v((R, 2048), BF16),
+        "dy_oh": v((8, R, 256), BF16), "pd_oh": v((8, R, 256), BF16), "mm": v((8, 32, 256), BF16),
+        "f": v((128, 1, 128), F32), "f_cr": v((64, 1, 128), F32), "f_a": v((64, 2, 128), F32),
+        "f_got": v((64, 2, 128), F32), "pd_first": v((3, 16, 17, 128), F32), "pd_b": v((16, 17, 128), F32),
         "ml": v((512, 1024), BF16), "mr": v((128, 1024), BF16), "vs": v((R, 256), BF16), "lg": v((272, R), BF16),
         "g": v((128, 1, 256), F32), "g_cr": v((64, 1, 256), F32), "g_a": v((64, 1, 256), F32),
         "g_got": v((64, 1, 256), F32),
     }
-    for name, extra in (("dy", 1), ("pd", 3)):
-        sent = 16 + min(extra, 2)
+    for name, slots in (("dy", 64), ("pd", 16)):
         shapes[name + "_own"] = v((16, R), BF16)
         shapes[name + "_loc"] = v((16, R), BF16)
         shapes[name + "_ob"] = v((128, R), BF16)
-        shapes[name + "_t"] = v((128, sent, 128), F32)
-        shapes[name + "_cr"] = v((64, sent, 128), F32)
-        shapes[name + "_a"] = v((64, 16 + extra, 128), F32)
-        shapes[name + "_got"] = v((64, 16 + extra, 128), F32)
+        shapes[name + "_t"] = v((128, 17, 128), F32)
+        shapes[name + "_cr"] = v((64, 17, 128), F32)
+        shapes[name + "_a"] = v((64, 17, 128), F32)
+        shapes[name + "_got"] = v((slots, 17, 128), F32)
         shapes[name + "_m"] = v((2, 64, 17, 128), F32)
+        shapes[name + "_mz"] = v((8, 2, 128), F32)
     shapes["send"] = pltpu.SemaphoreType.DMA((32,))
     shapes["recv"] = pltpu.SemaphoreType.DMA((32,))
     return shapes

time: 61.5 us -> 61.2 us (level)
  no operation moved by 1% of the time
where the time goes in v3:
time: 61.2 us; the launch traced here: 61 us
  Pallas kernels  55.2 us (90%)
  local copies, waits for them, and re-layouts  3.39 us (6%)
  between operations  2.46 us (4%)
    pallas_call x1, Pallas kernels, shards(): pl.pallas_call(functools.partial(kernel, total_rows), out_shape=(jax.Shap...  55.2 us
    unnamed x7, local copies, waits for them, and re-layouts  3.39 us

profile of v3, /device:TPU:1, one launch (start us, length us, event | category | flops | bytes accessed | tf_op | source)
XLA Modules:
  0.0 61.0 jit_solution(12031102149953671019)
XLA Ops:
  0.6 55.2 %demean.1 = (f32[2048,128]{1,0:T(8,128)}, f32[1,2048]{1,0:T(1,128)}, f32[1,128]{1,0:T(1,128)}, f32[1,1]{1,0:T(1,128)}) custom-call(f32[2048,128]{1,0:T(8,128)} %x_ref.1, f32[1,2048]{1,0:T(1,128)} %bitcast.23, f32[1,2048]{1,0:T(1,128)} %bitcast.13, s32[1,2048]{1,0:T(1,128)} %bitcast.15, s32[1,2048]{1,0:T(1,128)} %bitcast.17, s32[1,2048]{1,0:T(1,128)} %bitcast.19, ...), custom_call_target="tpu_custom_call" | custom-call | tf_op jit(solution)/shard_map/demean/pallas_call | solution.py:472
  55.8 0.0 copy-start
  55.8 2.3 %copy.15 = f32[2048,128]{1,0:T(8,128)} copy(f32[2048,128]{1,0:T(8,128)} %get-tuple-element.16) | data formatting | bytes 2097152
  58.1 0.0 copy-done
  58.1 0.0 copy-start.1
  58.1 0.6 copy.16
  58.7 0.0 copy-done.1
  58.7 0.5 copy.17
Async XLA Ops:
  55.8 2.3 %copy-start = (f32[1,2048]{1,0:T(1,128)S(1)}, f32[1,2048]{1,0:T(1,128)}, u32[]{:S(2)}) copy-start(f32[1,2048]{1,0:T(1,128)} %get-tuple-element.9) | copy-start | bytes 24580
  58.1 0.6 copy-start.1

commit v4 on v3

--- a/solution.py
+++ b/solution.py
@@ -295,14 +295,39 @@
                 s[name + "_oh"][t // 2, rows, blk(t % 2)] = (col == lane + 128.0 * t).astype(F32).astype(BF16)
 
     onehot_cols("dy")
+
+    for i in range(16):
+        v = s["v"][blk(i), :]
+        hi, lo = split2(v)
+        s["vs"][blk(i), 0:128] = hi
+        s["vs"][blk(i), 128:256] = lo
+        hi, lo = split2(jnp.transpose(v * s["wc"][blk(i), :]))
+        s["lg"][0:128, blk(i)] = hi
+        s["lg"][128:256, blk(i)] = lo
+    hi, lo = split2(wz_row)
+    row_id = iota((16, R), 0)
+    s["lg"][256:272, :] = jnp.where(
+        row_id == 0, hi.astype(F32), jnp.where(row_id == 1, lo.astype(F32), 0.0)).astype(BF16)
+    g = dot(s["lg"][...], s["vs"][...])
+    rhs_row = jnp.sum(g[256:272, 0:128] + g[256:272, 128:256], axis=0, keepdims=True)
+    g = g[0:128, 0:128] + g[0:128, 128:256] + g[128:256, 0:128] + g[128:256, 128:256]
+
+    def outer(a, b):
+        return lax.dot_general(a, b, (((0,), (0,)), ((), ())), precision=lax.Precision.HIGHEST,
+                               preferred_element_type=F32)
+
     dy_wait()
     total = jnp.sum(s["dy_got"][...], axis=0)
     row = total[16:17]
     w16 = column(row, 16)
     den = jnp.where(w16 > 0.0, w16, 1.0)
     lane_at = 16 * lax.rem(place, 8)
-    ag_dy = gather(s["dy_m"], jnp.concatenate([total[0:16] / den, as_row(column(row, 0) / den, lane_at)], axis=0))
+    mx = total[0:16] / den
+    m_z = column(row, 0) / den
+    ag_dy = gather(s["dy_m"], jnp.concatenate([mx, as_row(m_z, lane_at)], axis=0))
     next(ag_dy)
+    g = g - outer(mx * w16, mx)
+    rhs_row = rhs_row - jnp.sum(mx * w16 * m_z, axis=0, keepdims=True)
     onehot_cols("pd")
     f_wait()
 
@@ -314,9 +339,9 @@
     w_hi, w_lo = w_hi.astype(F32), w_lo.astype(F32)
     sub256 = iota((256, 128), 0)
     pair = jnp.zeros((512, 128), F32)
-    for g in range(4):
+    for step in range(4):
         for h in range(8):
-            t = g * 8 + h
+            t = step * 8 + h
             there = jnp.broadcast_to(high_t[t:t + 1], (256, 128)) == sub256
             s["ml"][0:256, blk(h)] = jnp.where(there, w_hi[t:t + 1], 0.0).astype(BF16)
             s["ml"][256:512, blk(h)] = jnp.where(there, w_lo[t:t + 1], 0.0).astype(BF16)
@@ -361,50 +386,8 @@
     qz = (column(pd_row, 0) - mmz) / den
     ag_pd = gather(s["pd_m"], jnp.concatenate([qx, as_row(qz, lane_at)], axis=0))
     next(ag_pd)
-
-    @pl.loop(0, 4)
-    def _(g):
-        rows = pl.ds(pl.multiple_of(g * 512, 512), 512)
-        got = jnp.zeros((512, 256), F32)
-        for k in range(8):
-            got += dot(s["dy_oh"][k, rows, :], s["mh"][blk(k, 256), :])
-        v = s["v"][rows, :] - (got[:, 0:128] + got[:, 128:256])
-        s["v"][rows, :] = v
-        xt_ref[rows, :] = v
-
-    def pick_z(index_row, mz):
-        high = lax.shift_right_logical(index_row, 7)
-        low = jnp.bitwise_and(index_row, 127)
-        parts = jnp.concatenate([v.astype(F32) for v in split3(mz)], axis=0).astype(BF16)
-        out = []
-        for i in range(16):
-            hot = (jnp.broadcast_to(low[:, blk(i)], (128, 128)) == sub).astype(F32).astype(BF16)
-            got = dot(parts, hot)
-            got = got[0:16] + got[16:32] + got[32:48]
-            out.append(jnp.sum(jnp.where(high[:, blk(i)] == sub_id, got, 0.0), axis=0, keepdims=True))
-        return jnp.concatenate(out, axis=1)
-
-    z_row = s["z"][...] - pick_z(dy_row, mz)
-
-    for i in range(16):
-        v = s["v"][blk(i), :]
-        hi, lo = split2(v)
-        s["vs"][blk(i), 0:128] = hi
-        s["vs"][blk(i), 128:256] = lo
-        hi, lo = split2(jnp.transpose(v * s["wc"][blk(i), :]))
-        s["lg"][0:128, blk(i)] = hi
-        s["lg"][128:256, blk(i)] = lo
-    hi, lo = split2(w_row * z_row)
-    row_id = iota((16, R), 0)
-    s["lg"][256:272, :] = jnp.where(
-        row_id == 0, hi.astype(F32), jnp.where(row_id == 1, lo.astype(F32), 0.0)).astype(BF16)
-    g = dot(s["lg"][...], s["vs"][...])
-    rhs_row = jnp.sum(g[256:272, 0:128] + g[256:272, 128:256], axis=0, keepdims=True)
-    g = g[0:128, 0:128] + g[0:128, 128:256] + g[128:256, 0:128] + g[128:256, 128:256]
-    wq = qx * w16
-    g = g - lax.dot_general(wq, qx, (((0,), (0,)), ((), ())), precision=lax.Precision.HIGHEST,
-                            preferred_element_type=F32)
-    rhs_row = rhs_row - jnp.sum(wq * qz, axis=0, keepdims=True)
+    g = g - outer(qx * w16, qx)
+    rhs_row = rhs_row - jnp.sum(qx * w16 * qz, axis=0, keepdims=True)
     eye = iota((128, 128), 0) == iota((128, 128), 1)
     rhs_col = jnp.sum(jnp.where(eye, rhs_row, 0.0), axis=1, keepdims=True)
     g = jnp.concatenate([g, jnp.broadcast_to(rhs_col, (128, 128))], axis=1)
@@ -418,14 +401,43 @@
     g_wait()
     s["g_a"][...] = s["g"][pl.ds(mine, 64)] + s["g_cr"][...]
     g_wait = scatter(s["g_a"], s["g_got"])
-    for half, first in ag_pd:
-        k, part = plane_halves("pd", half, first)
-
+
+    @pl.loop(0, 4)
+    def _(g):
+        rows = pl.ds(pl.multiple_of(g * 512, 512), 512)
+        got = jnp.zeros((512, 256), F32)
+        for k in range(8):
+            got += dot(s["dy_oh"][k, rows, :], s["mh"][blk(k, 256), :])
+        xt_ref[rows, :] = s["v"][rows, :] - (got[:, 0:128] + got[:, 128:256])
+
+    def pick_z(index_row, mz):
+        high = lax.shift_right_logical(index_row, 7)
+        low = jnp.bitwise_and(index_row, 127)
+        parts = jnp.concatenate([v.astype(F32) for v in split3(mz)], axis=0).astype(BF16)
+        out = []
+        for i in range(16):
+            hot = (jnp.broadcast_to(low[:, blk(i)], (128, 128)) == sub).astype(F32).astype(BF16)
+            got = dot(parts, hot)
+            got = got[0:16] + got[16:32] + got[32:48]
+            out.append(jnp.sum(jnp.where(high[:, blk(i)] == sub_id, got, 0.0), axis=0, keepdims=True))
+        return jnp.concatenate(out, axis=1)
+
+    z_row = s["z"][...] - pick_z(dy_row, mz)
+
+    def pick_half(half):
         @pl.loop(0, 4)
         def _(g):
             rows = pl.ds(pl.multiple_of(g * 512, 512), 512)
-            got = dot(s["pd_oh"][k, rows, :], s["mh"][part, :])
+            got = jnp.zeros((512, 256), F32)
+            for j in range(4):
+                part = pl.ds(pl.multiple_of(1024 * half + 256 * j, 256), 256)
+                got += dot(s["pd_oh"][4 * half + j, rows, :], s["mh"][part, :])
             xt_ref[rows, :] -= got[:, 0:128] + got[:, 128:256]
+
+    for i, (half, first) in enumerate(ag_pd):
+        plane_halves("pd", half, first)
+        if i in (3, 7):
+            pick_half(half)
 
     zt_ref[...] = z_row - pick_z(po_row * 16 + pl_row, s["pd_mz"][...].reshape(16, 128))
     g_wait()

time: 61.2 us -> 57.1 us (0.933)
  Pallas kernels: 55.2 us -> 51.1 us
    pallas_call x1, Pallas kernels: 55.2 us -> 51.1 us  [shards(): pl.pallas_call(functools.partial(kernel, total_rows), out_shape=(jax.Shap...]
where the time goes in v4:
time: 57.1 us; the launch traced here: 56.9 us
  Pallas kernels  51.1 us (89%)
  local copies, waits for them, and re-layouts  3.39 us (6%)
  between operations  2.46 us (4%)
    pallas_call x1, Pallas kernels, shards(): pl.pallas_call(functools.partial(kernel, total_rows), out_shape=(jax.Shap...  51.1 us
    unnamed x7, local copies, waits for them, and re-layouts  3.39 us

profile of v4, /device:TPU:1, one launch (start us, length us, event | category | flops | bytes accessed | tf_op | source)
XLA Modules:
  0.0 56.9 jit_solution(8969230474781992121)
XLA Ops:
  0.6 51.1 %demean.1 = (f32[2048,128]{1,0:T(8,128)}, f32[1,2048]{1,0:T(1,128)}, f32[1,128]{1,0:T(1,128)}, f32[1,1]{1,0:T(1,128)}) custom-call(f32[2048,128]{1,0:T(8,128)} %x_ref.1, f32[1,2048]{1,0:T(1,128)} %bitcast.23, f32[1,2048]{1,0:T(1,128)} %bitcast.13, s32[1,2048]{1,0:T(1,128)} %bitcast.15, s32[1,2048]{1,0:T(1,128)} %bitcast.17, s32[1,2048]{1,0:T(1,128)} %bitcast.19, ...), custom_call_target="tpu_custom_call" | custom-call | tf_op jit(solution)/shard_map/demean/pallas_call | solution.py:484
  51.7 0.0 copy-start
  51.8 2.3 %copy.15 = f32[2048,128]{1,0:T(8,128)} copy(f32[2048,128]{1,0:T(8,128)} %get-tuple-element.16) | data formatting | bytes 2097152
  54.0 0.0 copy-done
  54.0 0.0 copy-start.1
  54.0 0.6 %copy.16 = f32[2048]{0:T(1024)} copy(f32[2048]{0:T(1024)S(1)} %bitcast.24) | data formatting | bytes 16384
  54.6 0.0 copy-done.1
  54.6 0.5 copy.17
Async XLA Ops:
  51.7 2.3 %copy-start = (f32[1,2048]{1,0:T(1,128)S(1)}, f32[1,2048]{1,0:T(1,128)}, u32[]{:S(2)}) copy-start(f32[1,2048]{1,0:T(1,128)} %get-tuple-element.9) | copy-start | bytes 24580
  54.0 0.6 %copy-start.1 = (f32[1,128]{1,0:T(1,128)S(1)}, f32[1,128]{1,0:T(1,128)}, u32[]{:S(2)}) copy-start(f32[1,128]{1,0:T(1,128)} %get-tuple-element.18) | copy-start | bytes 1540

commit v5 on v4

--- a/solution.py
+++ b/solution.py
@@ -448,6 +448,20 @@
         wait()
 
 
+def put_out(x_in, z_in, g_in, r_in, x_out, z_out, g_out, r_out, x_buf, z_buf, g_buf, r_buf, sem_in, sem_out):
+    pairs = [(x_in.at[blk(i, 512)], x_buf.at[blk(i, 512)], x_out.at[blk(i, 512)]) for i in range(4)]
+    pairs += [(z_in, z_buf, z_out), (g_in, g_buf, g_out), (r_in, r_buf, r_out)]
+    loads = [pltpu.make_async_copy(src, buf, sem_in.at[i]) for i, (src, buf, _) in enumerate(pairs)]
+    stores = [pltpu.make_async_copy(buf, dst, sem_out.at[i]) for i, (_, buf, dst) in enumerate(pairs)]
+    for load in loads:
+        load.start()
+    for load, store in zip(loads, stores):
+        load.wait()
+        store.start()
+    for store in stores:
+        store.wait()
+
+
 def scratch():
     v = pltpu.VMEM
     shapes = {
@@ -492,6 +506,16 @@
             collective_id=0, has_side_effects=True, vmem_limit_bytes=63 * 1024 * 1024),
         name="demean",
     )(covariates, *rows, *squares)
+    xt, zt, gram, rhs = pl.pallas_call(
+        put_out,
+        out_shape=(jax.ShapeDtypeStruct((R, 128), F32), jax.ShapeDtypeStruct((1, R), F32),
+                   jax.ShapeDtypeStruct((1, 128), F32), jax.ShapeDtypeStruct((1, 1), F32)),
+        in_specs=[pl.BlockSpec(memory_space=pl.ANY)] * 4,
+        out_specs=[pl.BlockSpec(memory_space=pl.ANY)] * 4,
+        scratch_shapes=[pltpu.VMEM(n, F32) for n in ((R, 128), (1, R), (1, 128), (1, 1))]
+        + [pltpu.SemaphoreType.DMA((7,)), pltpu.SemaphoreType.DMA((7,))],
+        name="put_out",
+    )(xt, zt, gram, rhs)
     return xt, zt.reshape(R), gram, rhs.reshape(1)
 
 

time: 57.1 us -> 54.9 us (0.961)
  local copies, waits for them, and re-layouts: 3.39 us -> 0 us
  Pallas kernels: 51.1 us -> 54.1 us
  between operations: 2.46 us -> 0.64 us
    unnamed x7 -> x0, local copies, waits for them, and re-layouts: 3.39 us -> none
    pallas_call x0 -> x1, Pallas kernels: none -> 2.61 us  [shards(): pl.pallas_call(put_out, out_shape=(jax.ShapeDtypeStruct((R, 128), F32), j...]
where the time goes in v5:
time: 54.9 us; the launch traced here: 54.7 us
  Pallas kernels  54.1 us (99%)
  between operations  0.64 us (1%)
    pallas_call x1, Pallas kernels, shards(): pl.pallas_call(functools.partial(kernel, total_rows), out_shape=(jax.Shap...  51.5 us
    pallas_call x1, Pallas kernels, shards(): pl.pallas_call(put_out, out_shape=(jax.ShapeDtypeStruct((R, 128), F32), j...  2.61 us

profile of v5, /device:TPU:1, one launch (start us, length us, event | category | flops | bytes accessed | tf_op | source)
XLA Modules:
  0.0 54.7 jit_solution(14261072298438672431)
XLA Ops:
  0.6 51.5 %demean.1 = (f32[2048,128]{1,0:T(8,128)}, f32[1,2048]{1,0:T(1,128)}, f32[1,128]{1,0:T(1,128)}, f32[1,1]{1,0:T(1,128)}) custom-call(f32[2048,128]{1,0:T(8,128)} %x_ref.1, f32[1,2048]{1,0:T(1,128)} %bitcast.23, f32[1,2048]{1,0:T(1,128)} %bitcast.13, s32[1,2048]{1,0:T(1,128)} %bitcast.15, s32[1,2048]{1,0:T(1,128)} %bitcast.17, s32[1,2048]{1,0:T(1,128)} %bitcast.19, ...), custom_call_target="tpu_custom_call" | custom-call | tf_op jit(solution)/shard_map/demean/pallas_call | solution.py:498
  52.1 2.6 %put_out.1 = (f32[2048,128]{1,0:T(8,128)}, f32[1,2048]{1,0:T(1,128)}, f32[1,128]{1,0:T(1,128)}, f32[1,1]{1,0:T(1,128)}) custom-call(f32[2048,128]{1,0:T(8,128)} %get-tuple-element.12.x_in, f32[1,2048]{1,0:T(1,128)} %get-tuple-element.13.z_in, f32[1,128]{1,0:T(1,128)} %get-tuple-element.14.g_in, f32[1,1]{1,0:T(1,128)} %get-tuple-element.15.r_in), custom_call_target="tpu_custom_call" | custom-call | tf_op jit(solution)/shard_map/put_out/pallas_call | solution.py:509
